TPU v7x, 128 devices: a whole 4x4x4 slice. The times are simulated.
128 devices in a mesh: dp: 8 (over x, y_hi), blk: 16 (over z, y_lo, core).
Axes of the slice: x: 4, y: 4 (y_hi: 2, y_lo: 2; y = y_hi * 2 + y_lo), z: 4, core: 2. Of those that a mesh axis runs over, the one named last changes fastest.
Arguments:
- tokens: bfloat16 [5120, 3072], P(('dp', 'blk')), may hold values from -24 to 24
- expert_ids: int32 [5120, 2], P(('dp', 'blk')), may hold values from 0 to 7, as said below
- route_probs: float32 [5120, 2], P(('dp', 'blk')), may hold values from 0.2 to 1
- scale_exps: int32 [3], replicated, may hold values from -2 to 2
- w_gate: bfloat16 [3072, 8192], P(None, 'blk'), may hold values from -0.109375 to 0.109375
- w_up: bfloat16 [3072, 8192], P(None, 'blk'), may hold values from -0.109375 to 0.109375
- w_down: bfloat16 [8192, 3072], P('blk'), may hold values from -0.0625 to 0.0625
- out_grad: bfloat16 [5120, 3072], P(('dp', 'blk')), may hold values from -24 to 24
Outputs:
- mixed: bfloat16 [5120, 3072], P(('dp', 'blk'))
- input_grad: bfloat16 [5120, 3072], P(('dp', 'blk'))
- grad_gate: bfloat16 [3072, 8192], P('dp', 'blk')
- grad_up: bfloat16 [3072, 8192], P('dp', 'blk')
- grad_down: bfloat16 [8192, 3072], P('blk', 'dp')
Inputs may be any that keep to these rules, and one draw needn't show every extreme that they name: `expert_ids`: the tokens are those dispatched to expert 0: each row names expert 0 and one other expert; the layer computes expert 0.
All inputs are finite; a program needn't handle non-finite values.
Results may differ from a plain program's by a relative error of at most 0.019.
Values may be sent and summed in bfloat16 or wider, within the bound.
No kernel may reach another device: no remote copies, remote signals or barrier semaphores. Data moves between devices by JAX's collectives and lax.ppermute only.
A program may use at most 128 MiB of HBM per device.

v0:
```python
import jax
import jax.numpy as jnp
import numpy as np
from jax import lax
from jax.experimental import pallas as pl
from jax.experimental.pallas import tpu as pltpu
from jax.sharding import PartitionSpec as P

BF16 = jnp.bfloat16
F32 = jnp.float32

VMEM = pl.BlockSpec(memory_space=pltpu.VMEM)
SMEM = pl.BlockSpec(memory_space=pltpu.SMEM)
HBM = pl.BlockSpec(memory_space=pl.ANY)
GRANT = pltpu.CompilerParams(vmem_limit_bytes=14 * 2**20)


GRAY = {0: (0, 0), 1: (1, 0), 2: (1, 1), 3: (0, 1)}
UNGRAY = {uv: x for x, uv in GRAY.items()}


def blk_flip(dza, dzb, dyl, dcore):
    pairs = []
    for b in range(16):
        (za, zb), yl, core = GRAY[b // 4], (b // 2) % 2, b % 2
        z = UNGRAY[(za ^ dza, zb ^ dzb)]
        pairs.append((b, z * 4 + (yl ^ dyl) * 2 + (core ^ dcore)))
    return pairs


def dp_flip(du, dv, ds):
    pairs = []
    for d in range(8):
        u, v = GRAY[d // 2]
        pairs.append((d, UNGRAY[(u ^ du, v ^ dv)] * 2 + ((d % 2) ^ ds)))
    return pairs


def place_table():
    rows = np.zeros((8, 5), np.int32)
    for bits in range(4):
        for d, owner in dp_flip(bits >> 1, bits & 1, 0):
            rows[d, bits] = owner // 2
    rows[:, 4] = np.arange(8) % 2
    return rows


def send(value, dza=0, dzb=0, dyl=0, dcore=0):
    return lax.ppermute(value, "blk", blk_flip(dza, dzb, dyl, dcore))


def swap(value, du=0, dv=0, ds=0):
    return lax.ppermute(value, "dp", dp_flip(du, dv, ds))


def gather_blk(mine):
    beside = send(mine, dyl=1)
    a = send(mine, dza=1)
    b = send(mine, dzb=1)
    far = send(mine, dza=1, dzb=1)
    a_beside = send(beside, dza=1)
    b_beside = send(beside, dzb=1)
    far_beside = send(far, dyl=1)
    pieces = [mine, beside, b, b_beside, a, a_beside, far, far_beside]
    return pieces + [send(piece, dcore=1) for piece in pieces]


def total(*parts):
    return sum(part.astype(F32) for part in parts)


def scatter_blk(own, other):
    parts = [own, send(other, dcore=1)]
    for flip in ({"dza": 1}, {"dzb": 1}, {"dyl": 1}):
        half = parts[0].shape[0] // 2
        out = total(*(part[half:] for part in parts)).astype(BF16)
        parts = [part[:half] for part in parts] + [send(out, **flip)]
    return total(*parts)


def merge_rows(own, got):
    rows, d = own.shape
    n = rows // 8

    def body(own, got, near, far_a, far_b):
        near[...] = total(own[: 6 * n], got[: 6 * n]).astype(BF16)
        far_a[...] = total(own[6 * n : 7 * n], got[6 * n : 7 * n]).astype(BF16)
        far_b[...] = total(own[7 * n :], got[7 * n :]).astype(BF16)

    return pl.pallas_call(
        body,
        in_specs=[VMEM] * 2,
        out_specs=[VMEM] * 3,
        out_shape=[pltpu.VMEM((count * n, d), BF16) for count in (6, 1, 1)],
        cost_estimate=pl.CostEstimate(
            flops=rows * d, transcendentals=0, bytes_accessed=6 * rows * d
        ),
        compiler_params=GRANT,
    )(own, got)


def scatter_blk_both(own, other):
    got = send(other, dcore=1)
    n = own.shape[0] // 8
    near, far_a, far_b = merge_rows(own, got)
    rows = [near[i * n : (i + 1) * n] for i in range(6)]
    from_a = send(far_a, dza=1)
    from_b = send(far_b, dzb=1)
    b = jnp.concatenate([total(rows[2], from_a), total(rows[3])], axis=0).astype(BF16)
    a = jnp.concatenate([total(rows[4]), total(rows[5], from_b)], axis=0).astype(BF16)
    got_b = send(b, dzb=1)
    got_a = send(a, dza=1)
    out = total(rows[1], got_b[n:], got_a[n:]).astype(BF16)
    last = send(out, dyl=1)
    return total(rows[0], got_b[:n], got_a[:n], last)


def start_copies(pieces, target, sems):
    copies, at = [], 0
    for i, piece in enumerate(pieces):
        copies.append(
            pltpu.make_async_copy(piece, target.at[pl.ds(at, piece.shape[0])], sems.at[i])
        )
        at += piece.shape[0]
    for copy in copies:
        copy.start()
    return copies


def wgrad_cost(rows, ff, d):
    return pl.CostEstimate(
        flops=2 * rows * ff * d, transcendentals=0, bytes_accessed=2 * (rows * (ff + d) + ff * d)
    )


def wgrad_join(table, left, pieces):
    rows, ff = left.shape
    d = pieces[0].shape[1]
    n = len(pieces)

    def body(table, left, *refs):
        ins, (right, *outs), (left_t, sems) = refs[:n], refs[n : n + 5], refs[n + 5 :]
        copies = start_copies(ins, right, sems)
        left_t[...] = left[...].T
        for copy in copies:
            copy.wait()
        cut_x(table, left_t, right, *outs)

    part = pltpu.VMEM((ff // 2, d // 2), BF16)
    return pl.pallas_call(
        body,
        in_specs=[SMEM, VMEM] + [HBM] * n,
        out_specs=[VMEM] * 5,
        out_shape=[pltpu.VMEM((rows, d), BF16)] + [part] * 4,
        scratch_shapes=[pltpu.VMEM((ff, rows), BF16), pltpu.SemaphoreType.DMA((n,))],
        cost_estimate=wgrad_cost(rows, ff, d),
        compiler_params=GRANT,
    )(table, left, *pieces)


def chunk(right, table, j, wide):
    return right[:, pl.ds(pl.multiple_of(table[j] * wide, wide), wide)]


def cut_x(table, left_t, right, send_a, keep_a, send_b, keep_b):
    half, wide = left_t.shape[0] // 2, right.shape[1] // 4
    for j in range(4):
        u, v = j >> 1, j & 1
        value = jnp.dot(
            left_t[...], chunk(right, table, j, wide), preferred_element_type=F32
        ).astype(BF16)
        to_a = send_a if u else keep_a
        to_b = send_b if v else keep_b
        to_a[:, v * wide : (v + 1) * wide] = value[:half]
        to_b[:, u * wide : (u + 1) * wide] = value[half:]


def wgrad_x(table, left, right):
    rows, ff = left.shape
    d = right.shape[1]

    def body(table, left, right, send_a, keep_a, send_b, keep_b, left_t):
        left_t[...] = left[...].T
        cut_x(table, left_t, right, send_a, keep_a, send_b, keep_b)

    return pl.pallas_call(
        body,
        in_specs=[SMEM, VMEM, VMEM],
        out_specs=[VMEM] * 4,
        out_shape=[pltpu.VMEM((ff // 2, d // 2), BF16)] * 4,
        scratch_shapes=[pltpu.VMEM((ff, rows), BF16)],
        cost_estimate=wgrad_cost(rows, ff, d),
        compiler_params=GRANT,
    )(table, left, right)


def wgrad_y(table, left, right):
    rows, ff = left.shape
    d = right.shape[1]
    wide = d // 4
    n = wide // 2

    def body(table, left, right, out, keep, left_t):
        left_t[...] = left[...].T
        for j in range(4):
            cols = slice(j * n, (j + 1) * n)
            value = jnp.dot(
                left_t[...], chunk(right, table, j, wide), preferred_element_type=F32
            ).astype(BF16)

            @pl.when(table[4] == 0)
            def _():
                keep[:, cols] = value[:, :n]
                out[:, cols] = value[:, n:]

            @pl.when(table[4] != 0)
            def _():
                out[:, cols] = value[:, :n]
                keep[:, cols] = value[:, n:]

    return pl.pallas_call(
        body,
        in_specs=[SMEM, VMEM, VMEM],
        out_specs=[VMEM] * 2,
        out_shape=[pltpu.VMEM((ff, d // 2), BF16)] * 2,
        scratch_shapes=[pltpu.VMEM((ff, rows), BF16)],
        cost_estimate=wgrad_cost(rows, ff, d),
        compiler_params=GRANT,
    )(table, left, right)


def cut_sum(keep, got):
    half, n = keep.shape[0] // 2, keep.shape[1] // 4

    def body(keep, got, send_a, keep_a, send_b, keep_b):
        for j in range(4):
            u, v = j >> 1, j & 1
            cols = slice(j * n, (j + 1) * n)
            value = total(keep[:, cols], got[:, cols]).astype(BF16)
            to_a = send_a if u else keep_a
            to_b = send_b if v else keep_b
            to_a[:, v * n : (v + 1) * n] = value[:half]
            to_b[:, u * n : (u + 1) * n] = value[half:]

    return pl.pallas_call(
        body,
        in_specs=[VMEM] * 2,
        out_specs=[VMEM] * 4,
        out_shape=[pltpu.VMEM((half, 2 * n), BF16)] * 4,
        cost_estimate=pl.CostEstimate(
            flops=keep.size, transcendentals=0, bytes_accessed=6 * keep.size
        ),
        compiler_params=GRANT,
    )(keep, got)


def merge_send(keep_a, got_a, keep_b, got_b):
    rows, cols = keep_a.shape
    wide = cols // 2

    def body(keep_a, got_a, keep_b, got_b, out_a, out_b):
        out_a[...] = total(keep_a[:, wide:], got_a[:, wide:]).astype(BF16)
        out_b[...] = total(keep_b[:, wide:], got_b[:, wide:]).astype(BF16)

    return pl.pallas_call(
        body,
        in_specs=[VMEM] * 4,
        out_specs=[VMEM] * 2,
        out_shape=[pltpu.VMEM((rows, wide), BF16)] * 2,
        cost_estimate=pl.CostEstimate(
            flops=rows * cols, transcendentals=0, bytes_accessed=6 * rows * cols
        ),
        compiler_params=GRANT,
    )(keep_a, got_a, keep_b, got_b)


def merge_last(table, keep_a, got_a, two_a, keep_b, got_b, two_b):
    rows, cols = keep_a.shape
    n = cols // 4

    def body(table, keep_a, got_a, two_a, keep_b, got_b, two_b, first, last):
        for at, parts in enumerate(((keep_a, got_a, two_a), (keep_b, got_b, two_b))):
            cut = slice(at * rows, (at + 1) * rows)
            for yh in range(2):
                cols = slice(yh * n, (yh + 1) * n)
                value = total(*(part[:, cols] for part in parts))

                @pl.when(table[4] == yh)
                def _():
                    first[cut, :] = value

                @pl.when(table[4] != yh)
                def _():
                    last[cut, :] = value.astype(BF16)

    return pl.pallas_call(
        body,
        in_specs=[SMEM] + [VMEM] * 6,
        out_specs=[VMEM] * 2,
        out_shape=[pltpu.VMEM((2 * rows, n), F32), pltpu.VMEM((2 * rows, n), BF16)],
        cost_estimate=pl.CostEstimate(
            flops=rows * cols, transcendentals=0, bytes_accessed=9 * rows * cols
        ),
        compiler_params=GRANT,
    )(table, keep_a, got_a, two_a, keep_b, got_b, two_b)


def scatter_dp_x(parts, table, scale):
    send_a, keep_a, send_b, keep_b = parts
    got_a = swap(send_a, du=1)
    got_b = swap(send_b, dv=1)
    out_a, out_b = merge_send(keep_a, got_a, keep_b, got_b)
    two_a = swap(out_a, dv=1)
    two_b = swap(out_b, du=1)
    first, last = merge_last(table, keep_a, got_a, two_a, keep_b, got_b, two_b)
    got = swap(last, ds=1)
    return total(first, got) * scale


def scatter_dp_y(parts, scale):
    out, keep = parts
    n = out.shape[1] // 4
    got = swap(out, ds=1)
    send_a, keep_a, send_b, keep_b = cut_sum(keep, got)
    two_a = swap(send_a, du=1)
    two_b = swap(send_b, dv=1)
    out_a = total(keep_a[:, n:], two_a[:, n:]).astype(BF16)
    out_b = total(keep_b[:, n:], two_b[:, n:]).astype(BF16)
    three_a = swap(out_a, dv=1)
    three_b = swap(out_b, du=1)
    own_a = total(keep_a[:, :n], two_a[:, :n], three_a)
    own_b = total(keep_b[:, :n], two_b[:, :n], three_b)
    return jnp.concatenate([own_a, own_b], axis=0) * scale


def contract_cols(left, right):
    return lax.dot_general(left, right, (((1,), (1,)), ((), ())), preferred_element_type=F32)


def forward(scales, pieces, w_gate, w_up):
    n = len(pieces)
    rows = sum(piece.shape[0] for piece in pieces)
    d, ff = w_gate.shape
    wide = min(256, ff)

    def body(scales, w_gate, w_up, *refs):
        ins, (tokens, hidden, to_gate, to_up, sems) = refs[:n], refs[n:]
        for copy in start_copies(ins, tokens, sems):
            copy.wait()
        for at in range(0, ff, wide):
            cols = slice(at, at + wide)
            gate_pre = jnp.dot(tokens[...], w_gate[:, cols], preferred_element_type=F32) * scales[0]
            up_pre = jnp.dot(tokens[...], w_up[:, cols], preferred_element_type=F32) * scales[1]
            sig = jax.nn.sigmoid(gate_pre)
            silu = gate_pre * sig
            hidden[:, cols] = (silu * up_pre).astype(BF16)
            to_up[:, cols] = silu
            to_gate[:, cols] = up_pre * sig * (1.0 + gate_pre * (1.0 - sig))

    return pl.pallas_call(
        body,
        in_specs=[SMEM, VMEM, VMEM] + [HBM] * n,
        out_specs=[VMEM] * 4,
        out_shape=[
            pltpu.VMEM((rows, d), BF16),
            pltpu.VMEM((rows, ff), BF16),
            pltpu.VMEM((rows, ff), F32),
            pltpu.VMEM((rows, ff), F32),
        ],
        scratch_shapes=[pltpu.SemaphoreType.DMA((n,))],
        cost_estimate=pl.CostEstimate(
            flops=4 * rows * d * ff,
            transcendentals=rows * ff,
            bytes_accessed=4 * d * (rows + ff) + 10 * rows * ff,
        ),
        compiler_params=GRANT,
    )(scales, w_gate, w_up, *pieces)


def backward(scales, scaled, w_down, to_gate, to_up):
    rows, d = scaled.shape
    ff = w_down.shape[0]
    tall = rows // 2

    def body(scales, scaled, w_down, to_gate, to_up, d_gate, d_up):
        for at in range(0, rows, tall):
            cut = slice(at, at + tall)
            d_hidden = contract_cols(scaled[cut], w_down[...]) * scales[2]
            d_gate[cut] = (d_hidden * to_gate[cut]).astype(BF16)
            d_up[cut] = (d_hidden * to_up[cut]).astype(BF16)

    return pl.pallas_call(
        body,
        in_specs=[SMEM, VMEM, VMEM, VMEM, VMEM],
        out_specs=[VMEM] * 2,
        out_shape=[pltpu.VMEM((rows, ff), BF16)] * 2,
        cost_estimate=pl.CostEstimate(
            flops=2 * rows * d * ff,
            transcendentals=0,
            bytes_accessed=2 * d * (rows + ff) + 12 * rows * ff,
        ),
        compiler_params=GRANT,
    )(scales, scaled, w_down, to_gate, to_up)


def down(hidden, w_down):
    rows, ff = hidden.shape
    d = w_down.shape[1]
    half, wide = rows // 2, min(1024, d)

    def body(hidden, w_down, other, own):
        @pl.loop(0, d // wide)
        def _(i):
            cols = pl.ds(pl.multiple_of(i * wide, wide), wide)
            value = jnp.dot(hidden[...], w_down[:, cols], preferred_element_type=F32).astype(BF16)
            own[:, cols] = value[:half]
            other[:, cols] = value[half:]

    return pl.pallas_call(
        body,
        in_specs=[VMEM, VMEM],
        out_specs=[VMEM] * 2,
        out_shape=[pltpu.VMEM((half, d), BF16)] * 2,
        cost_estimate=pl.CostEstimate(
            flops=2 * rows * d * ff, transcendentals=0, bytes_accessed=2 * (rows + ff) * (d + ff)
        ),
        compiler_params=GRANT,
    )(hidden, w_down)


def back(scales, d_gate, d_up, w_gate, w_up):
    rows, ff = d_gate.shape
    d = w_gate.shape[0]
    half, wide = rows // 2, min(768, d)

    def body(scales, d_gate, d_up, w_gate, w_up, other, own):
        @pl.loop(0, d // wide)
        def _(i):
            cols = pl.ds(pl.multiple_of(i * wide, wide), wide)
            value = contract_cols(d_gate[...], w_gate[cols, :]) * scales[0]
            value = (value + contract_cols(d_up[...], w_up[cols, :]) * scales[1]).astype(BF16)
            own[:, cols] = value[:half]
            other[:, cols] = value[half:]

    return pl.pallas_call(
        body,
        in_specs=[SMEM] + [VMEM] * 4,
        out_specs=[VMEM] * 2,
        out_shape=[pltpu.VMEM((half, d), BF16)] * 2,
        cost_estimate=pl.CostEstimate(
            flops=4 * rows * d * ff,
            transcendentals=0,
            bytes_accessed=2 * rows * (d + 2 * ff) + 4 * d * ff,
        ),
        compiler_params=GRANT,
    )(scales, d_gate, d_up, w_gate, w_up)


def layer(tokens, expert_ids, route_probs, scale_exps, w_gate, w_up, w_down, out_grad):
    scales = jnp.exp2(scale_exps.astype(F32))
    combine = jnp.sum(jnp.where(expert_ids == 0, route_probs, jnp.zeros_like(route_probs)), axis=1)[
        :, None
    ]
    table = jnp.asarray(place_table())[lax.axis_index("dp")]
    scaled = (combine * out_grad.astype(F32)).astype(BF16)
    w_gate, w_up, w_down = (
        pltpu.with_memory_space_constraint(w, pltpu.VMEM) for w in (w_gate, w_up, w_down)
    )
    token_pieces = gather_blk(tokens)
    scaled_pieces = gather_blk(scaled)
    all_tokens, hidden, to_gate, to_up = forward(scales, token_pieces, w_gate, w_up)
    all_scaled, send_a, keep_a, send_b, keep_b = wgrad_join(table, hidden, scaled_pieces)
    later, combine_later, send_a = lax.optimization_barrier((hidden, combine, send_a))
    grad_down = scatter_dp_x((send_a, keep_a, send_b, keep_b), table, scales[2])

    d_gate, d_up = backward(scales, all_scaled, w_down, to_gate, to_up)
    grad_gate = scatter_dp_y(wgrad_y(table, d_gate, all_tokens), scales[0])
    send_a, keep_a, send_b, keep_b = wgrad_x(table, d_up, all_tokens)
    grad_up = scatter_dp_x((send_a, keep_a, send_b, keep_b), table, scales[1])

    other, own = down(later, w_down)
    expert_out = scatter_blk(own, other) * scales[2]
    mixed = (combine_later * expert_out).astype(BF16)
    other, own = back(scales, d_gate, d_up, w_gate, w_up)
    input_grad = scatter_blk_both(own, other)
    return (
        mixed,
        input_grad.astype(BF16),
        grad_gate.T.astype(BF16),
        grad_up.T.astype(BF16),
        grad_down.astype(BF16),
    )


def solution(mesh):
    return jax.shard_map(
        layer,
        mesh=mesh,
        in_specs=(
            P(("dp", "blk"), None),
            P(("dp", "blk"), None),
            P(("dp", "blk"), None),
            P(),
            P(None, "blk"),
            P(None, "blk"),
            P("blk", None),
            P(("dp", "blk"), None),
        ),
        out_specs=(
            P(("dp", "blk"), None),
            P(("dp", "blk"), None),
            P("dp", "blk"),
            P("dp", "blk"),
            P("blk", "dp"),
        ),
        check_vma=False,
    )
```

profile of v0, /device:TPU:4, one launch (start us, length us, event | category | flops | bytes accessed | tf_op | source)
XLA Modules:
  0.0 221.6 jit_solution(5370321466649772702)
XLA Ops:
  2.3 3.9 %collective-permute-start.5 = (bf16[40,3072]{1,0:T(8,128)(2,1)}, bf16[40,3072]{1,0:T(8,128)(2,1)S(1)}, u32[]{:S(2)}, u32[]{:S(2)}) collective-permute-start(bf16[40,3072]{1,0:T(8,128)(2,1)} %refs_0_.1), channel_id=1, source_target_pairs={{0,8},{1,9},{2,10},{3,11},{4,12},{5,13},{6,14},{7,15},{8,0},{9,1},... | collective-permute-start | bytes 737288 | tf_op jit(solution)/shard_map/ppermute | solution.py:49
  10.2 3.0 %collective-permute-done.5.refs_6_ = bf16[40,3072]{1,0:T(8,128)(2,1)S(1)} collective-permute-done((bf16[40,3072]{1,0:T(8,128)(2,1)}, bf16[40,3072]{1,0:T(8,128)(2,1)S(1)}, u32[]{:S(2)}, u32[]{:S(2)}) %collective-permute-start.5) | collective-permute-done | bytes 245792 | tf_op jit(solution)/shard_map/ppermute | solution.py:49
  13.2 3.5 %collective-permute-start.20 = (bf16[40,3072]{1,0:T(8,128)(2,1)S(1)}, bf16[40,3072]{1,0:T(8,128)(2,1)S(1)}, u32[]{:S(2)}, u32[]{:S(2)}) collective-permute-start(bf16[40,3072]{1,0:T(8,128)(2,1)S(1)} %multiply_convert_fusion.3.refs_0_), channel_id=1, source_target_pairs={{0,8},{1,9},{2,10},{3,11},{4,12},{5,13},{6,14},{7,15},{8,0},{9,1},... | collective-permute-start | bytes 737288 | tf_op jit(solution)/shard_map/ppermute | solution.py:49
  16.7 2.8 %collective-permute-done.3.refs_4_ = bf16[40,3072]{1,0:T(8,128)(2,1)S(1)} collective-permute-done((bf16[40,3072]{1,0:T(8,128)(2,1)}, bf16[40,3072]{1,0:T(8,128)(2,1)S(1)}, u32[]{:S(2)}, u32[]{:S(2)}) %collective-permute-start.3) | collective-permute-done | bytes 245792 | tf_op jit(solution)/shard_map/ppermute | solution.py:49
  20.6 2.6 %collective-permute-start.2 = (bf16[40,3072]{1,0:T(8,128)(2,1)S(1)}, bf16[40,3072]{1,0:T(8,128)(2,1)S(1)}, u32[]{:S(2)}, u32[]{:S(2)}) collective-permute-start(bf16[40,3072]{1,0:T(8,128)(2,1)S(1)} %collective-permute-done.refs_1_), channel_id=1, source_target_pairs={{0,12},{1,13},{2,14},{3,15},{4,8},{5,9},{6,10},{7,11},{8,4},{9,5},... | collective-permute-start | bytes 737288 | tf_op jit(solution)/shard_map/ppermute | solution.py:49
  24.4 5.2 %collective-permute-done.16.refs_2_ = bf16[40,3072]{1,0:T(8,128)(2,1)S(1)} collective-permute-done((bf16[40,3072]{1,0:T(8,128)(2,1)S(1)}, bf16[40,3072]{1,0:T(8,128)(2,1)S(1)}, u32[]{:S(2)}, u32[]{:S(2)}) %collective-permute-start.16) | collective-permute-done | bytes 245792 | tf_op jit(solution)/shard_map/ppermute | solution.py:49
  30.6 2.6 %collective-permute-done.2.refs_3_ = bf16[40,3072]{1,0:T(8,128)(2,1)S(1)} collective-permute-done((bf16[40,3072]{1,0:T(8,128)(2,1)S(1)}, bf16[40,3072]{1,0:T(8,128)(2,1)S(1)}, u32[]{:S(2)}, u32[]{:S(2)}) %collective-permute-start.2) | collective-permute-done | bytes 245792 | tf_op jit(solution)/shard_map/ppermute | solution.py:49
  35.7 3.3 %collective-permute-start.17 = (bf16[40,3072]{1,0:T(8,128)(2,1)S(1)}, bf16[40,3072]{1,0:T(8,128)(2,1)}, u32[]{:S(2)}, u32[]{:S(2)}) collective-permute-start(bf16[40,3072]{1,0:T(8,128)(2,1)S(1)} %collective-permute-done.15.refs_1_), channel_id=1, source_target_pairs={{0,12},{1,13},{2,14},{3,15},{4,8},{5,9},{6,10},{7,11},{8,4},{9,5},... | collective-permute-start | bytes 737288 | tf_op jit(solution)/shard_map/ppermute | solution.py:49
  41.5 2.8 %collective-permute-done.17.refs_3_ = bf16[40,3072]{1,0:T(8,128)(2,1)} collective-permute-done((bf16[40,3072]{1,0:T(8,128)(2,1)S(1)}, bf16[40,3072]{1,0:T(8,128)(2,1)}, u32[]{:S(2)}, u32[]{:S(2)}) %collective-permute-start.17) | collective-permute-done | bytes 245792 | tf_op jit(solution)/shard_map/ppermute | solution.py:49
  56.7 9.8 %shard_map.128 = (bf16[640,3072]{1,0:T(8,128)(2,1)S(1)}, bf16[640,512]{1,0:T(8,128)(2,1)S(1)}, f32[640,512]{1,0:T(8,128)S(1)}, f32[640,512]{1,0:T(8,128)S(1)}) custom-call(f32[3]{0:T(128)S(1)} %multiply_exponential_fusion.scales, bf16[3072,512]{1,0:T(8,128)(2,1)S(1)} %copy-done.7, bf16[3072,512]{1,0:T(8,128)(2,1)S(1)} %copy-done.9, ...), custom_call_target="tpu_custom_call" | custom-call | flops 4026531840 | bytes 17432576 | tf_op jit(solution)/shard_map/pallas_call | solution.py:360
  66.6 8.0 %shard_map.129 = (bf16[640,3072]{1,0:T(8,128)(2,1)S(1)}, bf16[256,1536]{1,0:T(8,128)(2,1)S(1)}, bf16[256,1536]{1,0:T(8,128)(2,1)S(1)}, bf16[256,1536]{1,0:T(8,128)(2,1)S(1)}, bf16[256,1536]{1,0:T(8,128)(2,1)S(1)}) custom-call(s32[5]{0:T(128)S(1)} %dynamic-slice_bitcast_fusion.table, bf16[640,512]{1,0:T(8,128)(2,1)S(1)} %get-tuple-element.47.left.hidden, ...), custom_call_target="tpu_custom_call" | custom-call | flops 2013265920 | bytes 7733248 | tf_op jit(solution)/shard_map/pallas_call | solution.py:150
  74.6 2.8 %shard_map.131 = (bf16[640,512]{1,0:T(8,128)(2,1)S(1)}, bf16[640,512]{1,0:T(8,128)(2,1)S(1)}) custom-call(f32[3]{0:T(128)S(1)} %multiply_exponential_fusion.scales, bf16[640,3072]{1,0:T(8,128)(2,1)S(1)} %get-tuple-element.50.scaled, bf16[512,3072]{1,0:T(8,128)(2,1)S(1)} %copy-done, f32[640,512]{1,0:T(8,128)S(1)} %get-tuple-element.51.to_gate, ...), custom_call_target="tpu_custom_call" | custom-call | flops 2013265920 | bytes 11010048 | tf_op jit(solution)/shard_map/pallas_call | solution.py:392
  77.4 3.2 %shard_map.136 = (bf16[256,1536]{1,0:T(8,128)(2,1)S(1)}, bf16[256,1536]{1,0:T(8,128)(2,1)S(1)}, bf16[256,1536]{1,0:T(8,128)(2,1)S(1)}, bf16[256,1536]{1,0:T(8,128)(2,1)S(1)}) custom-call(s32[5]{0:T(128)S(1)} %dynamic-slice_bitcast_fusion.table, bf16[640,512]{1,0:T(8,128)(2,1)S(1)} %get-tuple-element.54.d_up.left, bf16[640,3072]{1,0:T(8,128)(2,1)S(1)} %get-tuple-element.60.right), custom_call_target="tpu_custom_call" | custom-call | flops 2013265920 | bytes 7733248 | tf_op jit(solution)/shard_map/pallas_call | solution.py:186
  85.3 5.0 %shard_map.134 = (bf16[512,1536]{1,0:T(8,128)(2,1)S(1)}, bf16[512,1536]{1,0:T(8,128)(2,1)S(1)}) custom-call(s32[5]{0:T(128)S(1)} %dynamic-slice_bitcast_fusion.table, bf16[640,512]{1,0:T(8,128)(2,1)S(1)} %get-tuple-element.53.d_gate.left, bf16[640,3072]{1,0:T(8,128)(2,1)S(1)} %get-tuple-element.60.right), custom_call_target="tpu_custom_call" | custom-call | flops 2013265920 | bytes 7733248 | tf_op jit(solution)/shard_map/pallas_call | solution.py:221
  90.4 3.0 %collective-permute-start.40 = (bf16[512,1536]{1,0:T(8,128)(2,1)S(1)}, bf16[512,1536]{1,0:T(8,128)(2,1)S(1)}, u32[]{:S(2)}, u32[]{:S(2)}) collective-permute-start(bf16[512,1536]{1,0:T(8,128)(2,1)S(1)} %get-tuple-element.62), channel_id=1, source_target_pairs={{0,16},{16,0},{32,48},{48,32},{64,80},{80,64},{96,112},{112,96},{1... | collective-permute-start | bytes 4718600 | tf_op jit(solution)/shard_map/ppermute | solution.py:53
  93.4 7.7 %collective-permute-done.45.got_a = bf16[256,1536]{1,0:T(8,128)(2,1)S(1)} collective-permute-done((bf16[256,1536]{1,0:T(8,128)(2,1)S(1)}, bf16[256,1536]{1,0:T(8,128)(2,1)S(1)}, u32[]{:S(2)}, u32[]{:S(2)}) %collective-permute-start.45) | collective-permute-done | bytes 786464 | tf_op jit(solution)/shard_map/ppermute | solution.py:53
  102.6 6.8 %shard_map.132 = (bf16[320,3072]{1,0:T(8,128)(2,1)}, bf16[320,3072]{1,0:T(8,128)(2,1)S(1)}) custom-call(f32[3]{0:T(128)S(1)} %multiply_exponential_fusion.scales, bf16[640,512]{1,0:T(8,128)(2,1)S(1)} %get-tuple-element.53.d_gate.left, bf16[640,512]{1,0:T(8,128)(2,1)S(1)} %get-tuple-element.54.d_up.left, bf16[3072,512]{1,0:T(8,128)(2,1)S(1)} %copy-done.8, ...), custom_call_target="tpu_custom_call" | custom-call | flops 4026531840 | bytes 11534336 | tf_op jit(solution)/shard_map/pallas_call | solution.py:445
  109.4 3.8 %shard_map.130 = (bf16[320,3072]{1,0:T(8,128)(2,1)}, bf16[320,3072]{1,0:T(8,128)(2,1)S(1)}) custom-call(bf16[640,512]{1,0:T(8,128)(2,1)S(1)} %get-tuple-element.47.left.hidden, bf16[512,3072]{1,0:T(8,128)(2,1)S(1)} %copy-done), custom_call_target="tpu_custom_call" | custom-call | flops 2013265920 | bytes 8257536 | tf_op jit(solution)/shard_map/pallas_call | solution.py:419
  113.2 4.1 %collective-permute-done.50.got_a = bf16[256,1536]{1,0:T(8,128)(2,1)S(1)} collective-permute-done((bf16[256,1536]{1,0:T(8,128)(2,1)S(1)}, bf16[256,1536]{1,0:T(8,128)(2,1)S(1)}, u32[]{:S(2)}, u32[]{:S(2)}) %collective-permute-start.50) | collective-permute-done | bytes 786464 | tf_op jit(solution)/shard_map/ppermute | solution.py:53
  121.4 5.2 %collective-permute-done.47.two_a = bf16[256,768]{1,0:T(8,128)(2,1)S(1)} collective-permute-done((bf16[256,768]{1,0:T(8,128)(2,1)S(1)}, bf16[256,768]{1,0:T(8,128)(2,1)S(1)}, u32[]{:S(2)}, u32[]{:S(2)}) %collective-permute-start.47) | collective-permute-done | bytes 393248 | tf_op jit(solution)/shard_map/ppermute | solution.py:53
  131.4 5.3 %collective-permute-done.52.two_a = bf16[256,768]{1,0:T(8,128)(2,1)S(1)} collective-permute-done((bf16[256,768]{1,0:T(8,128)(2,1)S(1)}, bf16[256,768]{1,0:T(8,128)(2,1)S(1)}, u32[]{:S(2)}, u32[]{:S(2)}) %collective-permute-start.52) | collective-permute-done | bytes 393248 | tf_op jit(solution)/shard_map/ppermute | solution.py:53
  136.7 2.9 %collective-permute-start.49 = (bf16[512,384]{1,0:T(8,128)(2,1)S(1)}, bf16[512,384]{1,0:T(8,128)(2,1)S(1)}, u32[]{:S(2)}, u32[]{:S(2)}) collective-permute-start(bf16[512,384]{1,0:T(8,128)(2,1)S(1)} %get-tuple-element.74), channel_id=1, source_target_pairs={{0,16},{16,0},{32,48},{48,32},{64,80},{80,64},{96,112},{112,96},{1... | collective-permute-start | bytes 1179656 | tf_op jit(solution)/shard_map/ppermute | solution.py:53
  144.8 2.8 %collective-permute-start.41 = (bf16[256,768]{1,0:T(8,128)(2,1)}, bf16[256,768]{1,0:T(8,128)(2,1)}, u32[]{:S(2)}, u32[]{:S(2)}) collective-permute-start(bf16[256,768]{1,0:T(8,128)(2,1)} %get-tuple-element.64), channel_id=1, source_target_pairs={{0,32},{16,48},{32,0},{48,16},{64,96},{80,112},{96,64},{112,80},{1... | collective-permute-start | bytes 1179656 | tf_op jit(solution)/shard_map/ppermute | solution.py:53
  147.5 2.7 %collective-permute-done.49 = bf16[512,384]{1,0:T(8,128)(2,1)S(1)} collective-permute-done((bf16[512,384]{1,0:T(8,128)(2,1)S(1)}, bf16[512,384]{1,0:T(8,128)(2,1)S(1)}, u32[]{:S(2)}, u32[]{:S(2)}) %collective-permute-start.49) | collective-permute-done | bytes 393248 | tf_op jit(solution)/shard_map/ppermute | solution.py:53
  160.4 3.3 %collective-permute-done.43 = bf16[256,768]{1,0:T(8,128)(2,1)S(1)} collective-permute-done((bf16[256,768]{1,0:T(8,128)(2,1)}, bf16[256,768]{1,0:T(8,128)(2,1)S(1)}, u32[]{:S(2)}, u32[]{:S(2)}) %collective-permute-start.43) | collective-permute-done | bytes 393248 | tf_op jit(solution)/shard_map/ppermute | solution.py:53
  163.8 4.5 %collective-permute-start.44 = (bf16[256,384]{1,0:T(8,128)(2,1)S(1)}, bf16[256,384]{1,0:T(8,128)(2,1)S(1)}, u32[]{:S(2)}, u32[]{:S(2)}) collective-permute-start(bf16[256,384]{1,0:T(8,128)(2,1)S(1)} %add_convert_fusion.7), channel_id=1, source_target_pairs={{0,32},{16,48},{32,0},{48,16},{64,96},{80,112},{96,64},{112,80},{1... | collective-permute-start | bytes 589832 | tf_op jit(solution)/shard_map/ppermute | solution.py:53
  172.7 2.5 %add_convert_fusion = bf16[160,3072]{1,0:T(8,128)(2,1)} fusion(bf16[320,3072]{1,0:T(8,128)(2,1)} %collective-permute-done.30, bf16[320,3072]{1,0:T(8,128)(2,1)S(1)} %get-tuple-element.48), kind=kLoop, calls=%fused_computation | loop fusion | flops 1966080 | bytes 2949120 | tf_op jit(solution)/shard_map/convert_element_type | solution.py:76
  187.3 12.8 %collective-permute-done.31 = bf16[160,3072]{1,0:T(8,128)(2,1)} collective-permute-done((bf16[160,3072]{1,0:T(8,128)(2,1)}, bf16[160,3072]{1,0:T(8,128)(2,1)}, u32[]{:S(2)}, u32[]{:S(2)}) %collective-permute-start.31) | collective-permute-done | bytes 983072 | tf_op jit(solution)/shard_map/ppermute | solution.py:49
  201.5 2.9 %collective-permute-start.32 = (bf16[80,3072]{1,0:T(8,128)(2,1)S(1)}, bf16[80,3072]{1,0:T(8,128)(2,1)S(1)}, u32[]{:S(2)}, u32[]{:S(2)}) collective-permute-start(bf16[80,3072]{1,0:T(8,128)(2,1)S(1)} %add_convert_fusion.1), channel_id=1, source_target_pairs={{0,12},{1,13},{2,14},{3,15},{4,8},{5,9},{6,10},{7,11},{8,4},{9,5},... | collective-permute-start | bytes 1474568 | tf_op jit(solution)/shard_map/ppermute | solution.py:49
  205.9 5.7 %collective-permute-done.32 = bf16[80,3072]{1,0:T(8,128)(2,1)S(1)} collective-permute-done((bf16[80,3072]{1,0:T(8,128)(2,1)S(1)}, bf16[80,3072]{1,0:T(8,128)(2,1)S(1)}, u32[]{:S(2)}, u32[]{:S(2)}) %collective-permute-start.32) | collective-permute-done | bytes 491552 | tf_op jit(solution)/shard_map/ppermute | solution.py:49
  214.1 4.9 %collective-permute-done.33 = bf16[40,3072]{1,0:T(8,128)(2,1)S(1)} collective-permute-done((bf16[40,3072]{1,0:T(8,128)(2,1)S(1)}, bf16[40,3072]{1,0:T(8,128)(2,1)S(1)}, u32[]{:S(2)}, u32[]{:S(2)}) %collective-permute-start.33) | collective-permute-done | bytes 245792 | tf_op jit(solution)/shard_map/ppermute | solution.py:49
  219.1 2.5 %multiply_convert_fusion.2 = bf16[40,3072]{1,0:T(8,128)(2,1)} fusion(bf16[40,3072]{1,0:T(8,128)(2,1)S(1)} %collective-permute-done.33, bf16[80,3072]{1,0:T(8,128)(2,1)S(1)} %collective-permute-done.32, bf16[160,3072]{1,0:T(8,128)(2,1)} %collective-permute-done.31, bf16[320,3072]{1,0:T(8,128)(2,1)} %collective-permute-done.30, f32[]{:T(128)} %bitcast.3, ...), kind=kLoop, calls=%fused_computation.12 | loop fusion | flops 1474560 | bytes 1474724 | tf_op jit(solution)/shard_map/convert_element_type | solution.py:483
  (151 shorter events, 78.6 us)
Async XLA Ops:
  2.3 10.9 %collective-permute-start.5 = (bf16[40,3072]{1,0:T(8,128)(2,1)}, bf16[40,3072]{1,0:T(8,128)(2,1)S(1)}, u32[]{:S(2)}, u32[]{:S(2)}) collective-permute-start(bf16[40,3072]{1,0:T(8,128)(2,1)} %refs_0_.1), channel_id=1, source_target_pairs={{0,8},{1,9},{2,10},{3,11},{4,12},{5,13},{6,14},{7,15},{8,0},{9,1},... | collective-permute-start | bytes 737288 | tf_op jit(solution)/shard_map/ppermute | solution.py:49
  6.2 13.3 %collective-permute-start.3 = (bf16[40,3072]{1,0:T(8,128)(2,1)}, bf16[40,3072]{1,0:T(8,128)(2,1)S(1)}, u32[]{:S(2)}, u32[]{:S(2)}) collective-permute-start(bf16[40,3072]{1,0:T(8,128)(2,1)} %refs_0_.1), channel_id=1, source_target_pairs={{0,4},{1,5},{2,6},{3,7},{4,0},{5,1},{6,2},{7,3},{8,12},{9,13},{10,... | collective-permute-start | bytes 737288 | tf_op jit(solution)/shard_map/ppermute | solution.py:49
  7.2 12.3 %collective-permute-start.1 = (bf16[40,3072]{1,0:T(8,128)(2,1)}, bf16[40,3072]{1,0:T(8,128)(2,1)S(1)}, u32[]{:S(2)}, u32[]{:S(2)}) collective-permute-start(bf16[40,3072]{1,0:T(8,128)(2,1)} %refs_0_.1), channel_id=1, source_target_pairs={{0,12},{1,13},{2,14},{3,15},{4,8},{5,9},{6,10},{7,11},{8,4},{9,5},... | collective-permute-start | bytes 737288 | tf_op jit(solution)/shard_map/ppermute | solution.py:49
  7.2 13.4 %collective-permute-start.7 = (bf16[40,3072]{1,0:T(8,128)(2,1)}, bf16[40,3072]{1,0:T(8,128)(2,1)S(1)}, u32[]{:S(2)}, u32[]{:S(2)}) collective-permute-start(bf16[40,3072]{1,0:T(8,128)(2,1)} %refs_0_.1), channel_id=1, source_target_pairs={{0,1},{1,0},{2,3},{3,2},{4,5},{5,4},{6,7},{7,6},{8,9},{9,8},{10,11... | collective-permute-start | bytes 737288 | tf_op jit(solution)/shard_map/ppermute | solution.py:49
  9.0 11.7 %collective-permute-start.15 = (bf16[40,3072]{1,0:T(8,128)(2,1)S(1)}, bf16[40,3072]{1,0:T(8,128)(2,1)S(1)}, u32[]{:S(2)}, u32[]{:S(2)}) collective-permute-start(bf16[40,3072]{1,0:T(8,128)(2,1)S(1)} %multiply_convert_fusion.3.refs_0_), channel_id=1, source_target_pairs={{0,2},{1,3},{2,0},{3,1},{4,6},{5,7},{6,4},{7,5},{8,10},{9,11},{10,... | collective-permute-start | bytes 737288 | tf_op jit(solution)/shard_map/ppermute | solution.py:49
  13.2 10.1 %collective-permute-start.20 = (bf16[40,3072]{1,0:T(8,128)(2,1)S(1)}, bf16[40,3072]{1,0:T(8,128)(2,1)S(1)}, u32[]{:S(2)}, u32[]{:S(2)}) collective-permute-start(bf16[40,3072]{1,0:T(8,128)(2,1)S(1)} %multiply_convert_fusion.3.refs_0_), channel_id=1, source_target_pairs={{0,8},{1,9},{2,10},{3,11},{4,12},{5,13},{6,14},{7,15},{8,0},{9,1},... | collective-permute-start | bytes 737288 | tf_op jit(solution)/shard_map/ppermute | solution.py:49
  19.5 10.6 %collective-permute-start.18 = (bf16[40,3072]{1,0:T(8,128)(2,1)S(1)}, bf16[40,3072]{1,0:T(8,128)(2,1)S(1)}, u32[]{:S(2)}, u32[]{:S(2)}) collective-permute-start(bf16[40,3072]{1,0:T(8,128)(2,1)S(1)} %multiply_convert_fusion.3.refs_0_), channel_id=1, source_target_pairs={{0,4},{1,5},{2,6},{3,7},{4,0},{5,1},{6,2},{7,3},{8,12},{9,13},{10,... | collective-permute-start | bytes 737288 | tf_op jit(solution)/shard_map/ppermute | solution.py:49
  20.6 12.5 %collective-permute-start.2 = (bf16[40,3072]{1,0:T(8,128)(2,1)S(1)}, bf16[40,3072]{1,0:T(8,128)(2,1)S(1)}, u32[]{:S(2)}, u32[]{:S(2)}) collective-permute-start(bf16[40,3072]{1,0:T(8,128)(2,1)S(1)} %collective-permute-done.refs_1_), channel_id=1, source_target_pairs={{0,12},{1,13},{2,14},{3,15},{4,8},{5,9},{6,10},{7,11},{8,4},{9,5},... | collective-permute-start | bytes 737288 | tf_op jit(solution)/shard_map/ppermute | solution.py:49
  23.3 10.6 %collective-permute-start.4 = (bf16[40,3072]{1,0:T(8,128)(2,1)S(1)}, bf16[40,3072]{1,0:T(8,128)(2,1)S(1)}, u32[]{:S(2)}, u32[]{:S(2)}) collective-permute-start(bf16[40,3072]{1,0:T(8,128)(2,1)S(1)} %collective-permute-done.refs_1_), channel_id=1, source_target_pairs={{0,4},{1,5},{2,6},{3,7},{4,0},{5,1},{6,2},{7,3},{8,12},{9,13},{10,... | collective-permute-start | bytes 737288 | tf_op jit(solution)/shard_map/ppermute | solution.py:49
  48.5 18.0 %collective-permute-start.24 = (bf16[40,3072]{1,0:T(8,128)(2,1)S(1)}, bf16[40,3072]{1,0:T(8,128)(2,1)S(1)}, u32[]{:S(2)}, u32[]{:S(2)}) collective-permute-start(bf16[40,3072]{1,0:T(8,128)(2,1)S(1)} %collective-permute-done.16.refs_2_), channel_id=1, source_target_pairs={{0,1},{1,0},{2,3},{3,2},{4,5},{5,4},{6,7},{7,6},{8,9},{9,8},{10,11... | collective-permute-start | bytes 737288 | tf_op jit(solution)/shard_map/ppermute | solution.py:49
  49.0 17.5 %collective-permute-start.26 = (bf16[40,3072]{1,0:T(8,128)(2,1)S(1)}, bf16[40,3072]{1,0:T(8,128)(2,1)S(1)}, u32[]{:S(2)}, u32[]{:S(2)}) collective-permute-start(bf16[40,3072]{1,0:T(8,128)(2,1)S(1)} %collective-permute-done.18.refs_4_), channel_id=1, source_target_pairs={{0,1},{1,0},{2,3},{3,2},{4,5},{5,4},{6,7},{7,6},{8,9},{9,8},{10,11... | collective-permute-start | bytes 737288 | tf_op jit(solution)/shard_map/ppermute | solution.py:49
  49.1 17.4 %collective-permute-start.25 = (bf16[40,3072]{1,0:T(8,128)(2,1)}, bf16[40,3072]{1,0:T(8,128)(2,1)S(1)}, u32[]{:S(2)}, u32[]{:S(2)}) collective-permute-start(bf16[40,3072]{1,0:T(8,128)(2,1)} %collective-permute-done.17.refs_3_), channel_id=1, source_target_pairs={{0,1},{1,0},{2,3},{3,2},{4,5},{5,4},{6,7},{7,6},{8,9},{9,8},{10,11... | collective-permute-start | bytes 737288 | tf_op jit(solution)/shard_map/ppermute | solution.py:49
  49.5 17.0 %collective-permute-start.27 = (bf16[40,3072]{1,0:T(8,128)(2,1)}, bf16[40,3072]{1,0:T(8,128)(2,1)S(1)}, u32[]{:S(2)}, u32[]{:S(2)}) collective-permute-start(bf16[40,3072]{1,0:T(8,128)(2,1)} %collective-permute-done.19.refs_5_), channel_id=1, source_target_pairs={{0,1},{1,0},{2,3},{3,2},{4,5},{5,4},{6,7},{7,6},{8,9},{9,8},{10,11... | collective-permute-start | bytes 737288 | tf_op jit(solution)/shard_map/ppermute | solution.py:49
  49.6 16.9 %collective-permute-start.29 = (bf16[40,3072]{1,0:T(8,128)(2,1)}, bf16[40,3072]{1,0:T(8,128)(2,1)S(1)}, u32[]{:S(2)}, u32[]{:S(2)}) collective-permute-start(bf16[40,3072]{1,0:T(8,128)(2,1)} %collective-permute-done.21.refs_7_), channel_id=1, source_target_pairs={{0,1},{1,0},{2,3},{3,2},{4,5},{5,4},{6,7},{7,6},{8,9},{9,8},{10,11... | collective-permute-start | bytes 737288 | tf_op jit(solution)/shard_map/ppermute | solution.py:49
  80.6 20.5 %collective-permute-start.45 = (bf16[256,1536]{1,0:T(8,128)(2,1)S(1)}, bf16[256,1536]{1,0:T(8,128)(2,1)S(1)}, u32[]{:S(2)}, u32[]{:S(2)}) collective-permute-start(bf16[256,1536]{1,0:T(8,128)(2,1)S(1)} %get-tuple-element.68), channel_id=1, source_target_pairs={{0,32},{16,48},{32,0},{48,16},{64,96},{80,112},{96,64},{112,80},{1... | collective-permute-start | bytes 2359304 | tf_op jit(solution)/shard_map/ppermute | solution.py:53
  81.9 20.4 %collective-permute-start.46 = (bf16[256,1536]{1,0:T(8,128)(2,1)S(1)}, bf16[256,1536]{1,0:T(8,128)(2,1)S(1)}, u32[]{:S(2)}, u32[]{:S(2)}) collective-permute-start(bf16[256,1536]{1,0:T(8,128)(2,1)S(1)} %get-tuple-element.70), channel_id=1, source_target_pairs={{0,96},{16,112},{32,64},{48,80},{64,32},{80,48},{96,0},{112,16},{1... | collective-permute-start | bytes 2359304 | tf_op jit(solution)/shard_map/ppermute | solution.py:53
  81.9 35.4 %collective-permute-start.50 = (bf16[256,1536]{1,0:T(8,128)(2,1)S(1)}, bf16[256,1536]{1,0:T(8,128)(2,1)S(1)}, u32[]{:S(2)}, u32[]{:S(2)}) collective-permute-start(bf16[256,1536]{1,0:T(8,128)(2,1)S(1)} %get-tuple-element.76), channel_id=1, source_target_pairs={{0,32},{16,48},{32,0},{48,16},{64,96},{80,112},{96,64},{112,80},{1... | collective-permute-start | bytes 2359304 | tf_op jit(solution)/shard_map/ppermute | solution.py:53
  83.9 35.3 %collective-permute-start.51 = (bf16[256,1536]{1,0:T(8,128)(2,1)S(1)}, bf16[256,1536]{1,0:T(8,128)(2,1)S(1)}, u32[]{:S(2)}, u32[]{:S(2)}) collective-permute-start(bf16[256,1536]{1,0:T(8,128)(2,1)S(1)} %get-tuple-element.78), channel_id=1, source_target_pairs={{0,96},{16,112},{32,64},{48,80},{64,32},{80,48},{96,0},{112,16},{1... | collective-permute-start | bytes 2359304 | tf_op jit(solution)/shard_map/ppermute | solution.py:53
  90.4 52.8 %collective-permute-start.40 = (bf16[512,1536]{1,0:T(8,128)(2,1)S(1)}, bf16[512,1536]{1,0:T(8,128)(2,1)S(1)}, u32[]{:S(2)}, u32[]{:S(2)}) collective-permute-start(bf16[512,1536]{1,0:T(8,128)(2,1)S(1)} %get-tuple-element.62), channel_id=1, source_target_pairs={{0,16},{16,0},{32,48},{48,32},{64,80},{80,64},{96,112},{112,96},{1... | collective-permute-start | bytes 4718600 | tf_op jit(solution)/shard_map/ppermute | solution.py:53
  102.5 24.1 %collective-permute-start.47 = (bf16[256,768]{1,0:T(8,128)(2,1)S(1)}, bf16[256,768]{1,0:T(8,128)(2,1)S(1)}, u32[]{:S(2)}, u32[]{:S(2)}) collective-permute-start(bf16[256,768]{1,0:T(8,128)(2,1)S(1)} %get-tuple-element.71), channel_id=1, source_target_pairs={{0,96},{16,112},{32,64},{48,80},{64,32},{80,48},{96,0},{112,16},{1... | collective-permute-start | bytes 1179656 | tf_op jit(solution)/shard_map/ppermute | solution.py:53
  109.4 59.0 %collective-permute-start.34 = (bf16[320,3072]{1,0:T(8,128)(2,1)}, bf16[320,3072]{1,0:T(8,128)(2,1)}, u32[]{:S(2)}, u32[]{:S(2)}) collective-permute-start(bf16[320,3072]{1,0:T(8,128)(2,1)} %get-tuple-element.56), channel_id=1, source_target_pairs={{0,1},{1,0},{2,3},{3,2},{4,5},{5,4},{6,7},{7,6},{8,9},{9,8},{10,11... | collective-permute-start | bytes 5898248 | tf_op jit(solution)/shard_map/ppermute | solution.py:49
  117.3 55.5 %collective-permute-start.30 = (bf16[320,3072]{1,0:T(8,128)(2,1)}, bf16[320,3072]{1,0:T(8,128)(2,1)}, u32[]{:S(2)}, u32[]{:S(2)}) collective-permute-start(bf16[320,3072]{1,0:T(8,128)(2,1)} %get-tuple-element.49), channel_id=1, source_target_pairs={{0,1},{1,0},{2,3},{3,2},{4,5},{5,4},{6,7},{7,6},{8,9},{9,8},{10,11... | collective-permute-start | bytes 5898248 | tf_op jit(solution)/shard_map/ppermute | solution.py:49
  126.6 10.1 %collective-permute-start.52 = (bf16[256,768]{1,0:T(8,128)(2,1)S(1)}, bf16[256,768]{1,0:T(8,128)(2,1)S(1)}, u32[]{:S(2)}, u32[]{:S(2)}) collective-permute-start(bf16[256,768]{1,0:T(8,128)(2,1)S(1)} %get-tuple-element.79), channel_id=1, source_target_pairs={{0,96},{16,112},{32,64},{48,80},{64,32},{80,48},{96,0},{112,16},{1... | collective-permute-start | bytes 1179656 | tf_op jit(solution)/shard_map/ppermute | solution.py:53
  128.8 10.8 %collective-permute-start.53 = (bf16[256,768]{1,0:T(8,128)(2,1)S(1)}, bf16[256,768]{1,0:T(8,128)(2,1)S(1)}, u32[]{:S(2)}, u32[]{:S(2)}) collective-permute-start(bf16[256,768]{1,0:T(8,128)(2,1)S(1)} %get-tuple-element.80), channel_id=1, source_target_pairs={{0,32},{16,48},{32,0},{48,16},{64,96},{80,112},{96,64},{112,80},{1... | collective-permute-start | bytes 1179656 | tf_op jit(solution)/shard_map/ppermute | solution.py:53
  136.7 13.5 %collective-permute-start.49 = (bf16[512,384]{1,0:T(8,128)(2,1)S(1)}, bf16[512,384]{1,0:T(8,128)(2,1)S(1)}, u32[]{:S(2)}, u32[]{:S(2)}) collective-permute-start(bf16[512,384]{1,0:T(8,128)(2,1)S(1)} %get-tuple-element.74), channel_id=1, source_target_pairs={{0,16},{16,0},{32,48},{48,32},{64,80},{80,64},{96,112},{112,96},{1... | collective-permute-start | bytes 1179656 | tf_op jit(solution)/shard_map/ppermute | solution.py:53
  141.4 14.6 %collective-permute-start.54 = (bf16[512,384]{1,0:T(8,128)(2,1)}, bf16[512,384]{1,0:T(8,128)(2,1)}, u32[]{:S(2)}, u32[]{:S(2)}) collective-permute-start(bf16[512,384]{1,0:T(8,128)(2,1)} %get-tuple-element.82), channel_id=1, source_target_pairs={{0,16},{16,0},{32,48},{48,32},{64,80},{80,64},{96,112},{112,96},{1... | collective-permute-start | bytes 1179656 | tf_op jit(solution)/shard_map/ppermute | solution.py:53
  144.8 13.7 %collective-permute-start.41 = (bf16[256,768]{1,0:T(8,128)(2,1)}, bf16[256,768]{1,0:T(8,128)(2,1)}, u32[]{:S(2)}, u32[]{:S(2)}) collective-permute-start(bf16[256,768]{1,0:T(8,128)(2,1)} %get-tuple-element.64), channel_id=1, source_target_pairs={{0,32},{16,48},{32,0},{48,16},{64,96},{80,112},{96,64},{112,80},{1... | collective-permute-start | bytes 1179656 | tf_op jit(solution)/shard_map/ppermute | solution.py:53
  159.4 16.7 %collective-permute-start.42 = (bf16[256,384]{1,0:T(8,128)(2,1)S(1)}, bf16[256,384]{1,0:T(8,128)(2,1)S(1)}, u32[]{:S(2)}, u32[]{:S(2)}) collective-permute-start(bf16[256,384]{1,0:T(8,128)(2,1)S(1)} %add_convert_fusion.8), channel_id=1, source_target_pairs={{0,96},{16,112},{32,64},{48,80},{64,32},{80,48},{96,0},{112,16},{1... | collective-permute-start | bytes 589832 | tf_op jit(solution)/shard_map/ppermute | solution.py:53
  163.8 13.4 %collective-permute-start.44 = (bf16[256,384]{1,0:T(8,128)(2,1)S(1)}, bf16[256,384]{1,0:T(8,128)(2,1)S(1)}, u32[]{:S(2)}, u32[]{:S(2)}) collective-permute-start(bf16[256,384]{1,0:T(8,128)(2,1)S(1)} %add_convert_fusion.7), channel_id=1, source_target_pairs={{0,32},{16,48},{32,0},{48,16},{64,96},{80,112},{96,64},{112,80},{1... | collective-permute-start | bytes 589832 | tf_op jit(solution)/shard_map/ppermute | solution.py:53
  176.1 24.0 %collective-permute-start.31 = (bf16[160,3072]{1,0:T(8,128)(2,1)}, bf16[160,3072]{1,0:T(8,128)(2,1)}, u32[]{:S(2)}, u32[]{:S(2)}) collective-permute-start(bf16[160,3072]{1,0:T(8,128)(2,1)} %add_convert_fusion), channel_id=1, source_target_pairs={{0,4},{1,5},{2,6},{3,7},{4,0},{5,1},{6,2},{7,3},{8,12},{9,13},{10,... | collective-permute-start | bytes 2949128 | tf_op jit(solution)/shard_map/ppermute | solution.py:49
  183.6 20.8 %collective-permute-start.36 = (bf16[80,3072]{1,0:T(8,128)(2,1)S(1)}, bf16[80,3072]{1,0:T(8,128)(2,1)S(1)}, u32[]{:S(2)}, u32[]{:S(2)}) collective-permute-start(bf16[80,3072]{1,0:T(8,128)(2,1)S(1)} %pad_maximum_fusion), channel_id=1, source_target_pairs={{0,12},{1,13},{2,14},{3,15},{4,8},{5,9},{6,10},{7,11},{8,4},{9,5},... | collective-permute-start | bytes 1474568 | tf_op jit(solution)/shard_map/ppermute | solution.py:49
  185.8 19.4 %collective-permute-start.38 = (bf16[80,3072]{1,0:T(8,128)(2,1)S(1)}, bf16[80,3072]{1,0:T(8,128)(2,1)S(1)}, u32[]{:S(2)}, u32[]{:S(2)}) collective-permute-start(bf16[80,3072]{1,0:T(8,128)(2,1)S(1)} %pad_maximum_fusion.1), channel_id=1, source_target_pairs={{0,4},{1,5},{2,6},{3,7},{4,0},{5,1},{6,2},{7,3},{8,12},{9,13},{10,... | collective-permute-start | bytes 1474568 | tf_op jit(solution)/shard_map/ppermute | solution.py:49
  (41 other events, 288.9 us)
where the time goes:
time: 223 us; the launch traced here: 222 us
  waiting for transfers between devices  82.4 us (37%)
  starting transfers between devices  57.1 us (26%)
  Pallas kernels  45.8 us (21%)
  other arithmetic  20.5 us (9%)
  local copies, waits for them, and re-layouts  14.7 us (7%)
    ppermute x40, waiting for transfers between devices, send(): return lax.ppermute(value, 'blk', blk_flip(dza, dzb, dyl, dcore))  47.2 us
    ppermute x15, waiting for transfers between devices, swap(): return lax.ppermute(value, 'dp', dp_flip(du, dv, ds))  35.2 us
    ppermute x40, starting transfers between devices, send(): return lax.ppermute(value, 'blk', blk_flip(dza, dzb, dyl, dcore))  32.6 us
    ppermute x15, starting transfers between devices, swap(): return lax.ppermute(value, 'dp', dp_flip(du, dv, ds))  24.6 us
    unnamed x38, local copies, waits for them, and re-layouts  12.6 us
    pallas_call x1, Pallas kernels, forward(): pl.pallas_call(body, in_specs=[SMEM, VMEM, VMEM] + [HBM] * n, out_specs=[...  9.83 us
    pallas_call x1, Pallas kernels, wgrad_join(): pl.pallas_call(body, in_specs=[SMEM, VMEM] + [HBM] * n, out_specs=[VMEM]...  7.99 us
    pallas_call x1, Pallas kernels, back(): pl.pallas_call(body, in_specs=[SMEM] + [VMEM] * 4, out_specs=[VMEM] * 2,...  6.75 us
  transfers between devices with their start and end apart: 55, of which 26 were waited for; matrix products, arithmetic and copies ran while one was open for 11% of the time, Pallas kernels for 14%

commit v1 on v0

--- a/solution.py
+++ b/solution.py
@@ -11,7 +11,6 @@
 
 VMEM = pl.BlockSpec(memory_space=pltpu.VMEM)
 SMEM = pl.BlockSpec(memory_space=pltpu.SMEM)
-HBM = pl.BlockSpec(memory_space=pl.ANY)
 GRANT = pltpu.CompilerParams(vmem_limit_bytes=14 * 2**20)
 
 
@@ -115,16 +114,35 @@
     return total(rows[0], got_b[:n], got_a[:n], last)
 
 
-def start_copies(pieces, target, sems):
-    copies, at = [], 0
-    for i, piece in enumerate(pieces):
-        copies.append(
-            pltpu.make_async_copy(piece, target.at[pl.ds(at, piece.shape[0])], sems.at[i])
-        )
+def join(pieces, target):
+    at = 0
+    for piece in pieces:
+        target[at : at + piece.shape[0]] = piece[...]
         at += piece.shape[0]
-    for copy in copies:
-        copy.start()
-    return copies
+
+
+def load(*arrays):
+    n = len(arrays)
+
+    def body(*refs):
+        for i in range(n):
+            tall = arrays[i].shape[0] // 8
+
+            @pl.loop(0, 8)
+            def _(j):
+                cut = pl.ds(pl.multiple_of(j * tall, tall), tall)
+                refs[n + i][cut, :] = refs[i][cut, :]
+
+    return pl.pallas_call(
+        body,
+        in_specs=[VMEM] * n,
+        out_specs=[VMEM] * n,
+        out_shape=[pltpu.VMEM(array.shape, array.dtype) for array in arrays],
+        cost_estimate=pl.CostEstimate(
+            flops=0, transcendentals=0, bytes_accessed=2 * sum(array.size for array in arrays)
+        ),
+        compiler_params=GRANT,
+    )(*arrays)
 
 
 def wgrad_cost(rows, ff, d):
@@ -139,20 +157,18 @@
     n = len(pieces)
 
     def body(table, left, *refs):
-        ins, (right, *outs), (left_t, sems) = refs[:n], refs[n : n + 5], refs[n + 5 :]
-        copies = start_copies(ins, right, sems)
+        ins, (right, *outs), left_t = refs[:n], refs[n : n + 5], refs[n + 5]
+        join(ins, right)
         left_t[...] = left[...].T
-        for copy in copies:
-            copy.wait()
         cut_x(table, left_t, right, *outs)
 
     part = pltpu.VMEM((ff // 2, d // 2), BF16)
     return pl.pallas_call(
         body,
-        in_specs=[SMEM, VMEM] + [HBM] * n,
+        in_specs=[SMEM, VMEM] + [VMEM] * n,
         out_specs=[VMEM] * 5,
         out_shape=[pltpu.VMEM((rows, d), BF16)] + [part] * 4,
-        scratch_shapes=[pltpu.VMEM((ff, rows), BF16), pltpu.SemaphoreType.DMA((n,))],
+        scratch_shapes=[pltpu.VMEM((ff, rows), BF16)],
         cost_estimate=wgrad_cost(rows, ff, d),
         compiler_params=GRANT,
     )(table, left, *pieces)
@@ -305,7 +321,37 @@
     )(table, keep_a, got_a, two_a, keep_b, got_b, two_b)
 
 
-def scatter_dp_x(parts, table, scale):
+def finish(scales, k, parts, flip):
+    n = parts[0][-1].shape[1]
+    rows = sum(block[-1].shape[0] for block in parts)
+    flat = [part for block in parts for part in block]
+
+    def body(scales, *refs):
+        refs, out = list(refs[:-1]), refs[-1]
+        at = 0
+        for block in parts:
+            some = [refs.pop(0)[:, :n] for _ in block]
+            value = (total(*some) * scales[k]).astype(BF16)
+            cut = slice(at, at + value.shape[0])
+            if flip:
+                out[:, cut] = value.T
+            else:
+                out[cut, :] = value
+            at += value.shape[0]
+
+    return pl.pallas_call(
+        body,
+        in_specs=[SMEM] + [VMEM] * len(flat),
+        out_specs=VMEM,
+        out_shape=jax.ShapeDtypeStruct((n, rows) if flip else (rows, n), BF16),
+        cost_estimate=pl.CostEstimate(
+            flops=3 * rows * n, transcendentals=0, bytes_accessed=8 * rows * n
+        ),
+        compiler_params=GRANT,
+    )(scales, *flat)
+
+
+def scatter_dp_x(parts, table, scales, k, flip):
     send_a, keep_a, send_b, keep_b = parts
     got_a = swap(send_a, du=1)
     got_b = swap(send_b, dv=1)
@@ -314,10 +360,10 @@
     two_b = swap(out_b, du=1)
     first, last = merge_last(table, keep_a, got_a, two_a, keep_b, got_b, two_b)
     got = swap(last, ds=1)
-    return total(first, got) * scale
-
-
-def scatter_dp_y(parts, scale):
+    return finish(scales, k, [[first, got]], flip)
+
+
+def scatter_dp_y(parts, scales, k, flip):
     out, keep = parts
     n = out.shape[1] // 4
     got = swap(out, ds=1)
@@ -328,9 +374,7 @@
     out_b = total(keep_b[:, n:], two_b[:, n:]).astype(BF16)
     three_a = swap(out_a, dv=1)
     three_b = swap(out_b, du=1)
-    own_a = total(keep_a[:, :n], two_a[:, :n], three_a)
-    own_b = total(keep_b[:, :n], two_b[:, :n], three_b)
-    return jnp.concatenate([own_a, own_b], axis=0) * scale
+    return finish(scales, k, [[keep_a, two_a, three_a], [keep_b, two_b, three_b]], flip)
 
 
 def contract_cols(left, right):
@@ -344,9 +388,8 @@
     wide = min(256, ff)
 
     def body(scales, w_gate, w_up, *refs):
-        ins, (tokens, hidden, to_gate, to_up, sems) = refs[:n], refs[n:]
-        for copy in start_copies(ins, tokens, sems):
-            copy.wait()
+        ins, (tokens, hidden, to_gate, to_up) = refs[:n], refs[n:]
+        join(ins, tokens)
         for at in range(0, ff, wide):
             cols = slice(at, at + wide)
             gate_pre = jnp.dot(tokens[...], w_gate[:, cols], preferred_element_type=F32) * scales[0]
@@ -359,7 +402,7 @@
 
     return pl.pallas_call(
         body,
-        in_specs=[SMEM, VMEM, VMEM] + [HBM] * n,
+        in_specs=[SMEM, VMEM, VMEM] + [VMEM] * n,
         out_specs=[VMEM] * 4,
         out_shape=[
             pltpu.VMEM((rows, d), BF16),
@@ -367,7 +410,6 @@
             pltpu.VMEM((rows, ff), F32),
             pltpu.VMEM((rows, ff), F32),
         ],
-        scratch_shapes=[pltpu.SemaphoreType.DMA((n,))],
         cost_estimate=pl.CostEstimate(
             flops=4 * rows * d * ff,
             transcendentals=rows * ff,
@@ -463,20 +505,21 @@
     ]
     table = jnp.asarray(place_table())[lax.axis_index("dp")]
     scaled = (combine * out_grad.astype(F32)).astype(BF16)
+    w_gate_now, w_up_now = load(w_gate)[0], load(w_up)[0]
     w_gate, w_up, w_down = (
         pltpu.with_memory_space_constraint(w, pltpu.VMEM) for w in (w_gate, w_up, w_down)
     )
     token_pieces = gather_blk(tokens)
     scaled_pieces = gather_blk(scaled)
-    all_tokens, hidden, to_gate, to_up = forward(scales, token_pieces, w_gate, w_up)
+    all_tokens, hidden, to_gate, to_up = forward(scales, token_pieces, w_gate_now, w_up_now)
     all_scaled, send_a, keep_a, send_b, keep_b = wgrad_join(table, hidden, scaled_pieces)
     later, combine_later, send_a = lax.optimization_barrier((hidden, combine, send_a))
-    grad_down = scatter_dp_x((send_a, keep_a, send_b, keep_b), table, scales[2])
+    grad_down = scatter_dp_x((send_a, keep_a, send_b, keep_b), table, scales, 2, False)
 
     d_gate, d_up = backward(scales, all_scaled, w_down, to_gate, to_up)
-    grad_gate = scatter_dp_y(wgrad_y(table, d_gate, all_tokens), scales[0])
+    grad_gate = scatter_dp_y(wgrad_y(table, d_gate, all_tokens), scales, 0, True)
     send_a, keep_a, send_b, keep_b = wgrad_x(table, d_up, all_tokens)
-    grad_up = scatter_dp_x((send_a, keep_a, send_b, keep_b), table, scales[1])
+    grad_up = scatter_dp_x((send_a, keep_a, send_b, keep_b), table, scales, 1, True)
 
     other, own = down(later, w_down)
     expert_out = scatter_blk(own, other) * scales[2]
@@ -486,9 +529,9 @@
     return (
         mixed,
         input_grad.astype(BF16),
-        grad_gate.T.astype(BF16),
-        grad_up.T.astype(BF16),
-        grad_down.astype(BF16),
+        grad_gate,
+        grad_up,
+        grad_down,
     )
 
 

time: 223 us -> 196 us (0.88)
  other arithmetic: 20.5 us -> 5.09 us
  Pallas kernels: 45.8 us -> 36.7 us
  local copies, waits for them, and re-layouts: 14.7 us -> 6.7 us
  waiting for transfers between devices: 82.4 us -> 90.1 us
  starting transfers between devices: 57.1 us -> 53.8 us
    ppermute x40, waiting for transfers between devices: 47.2 us -> 58.5 us  [send(): return lax.ppermute(value, 'blk', blk_flip(dza, dzb, dyl, dcore))]
    unnamed x38 -> x24, local copies, waits for them, and re-layouts: 12.6 us -> 5.36 us
    convert_element_type x4 -> x1, other arithmetic: 6.1 us -> 0.82 us  [layer(): return (mixed, input_grad.astype(BF16), grad_gate, grad_up, grad_down)]
    ppermute x40, starting transfers between devices: 32.6 us -> 27.9 us  [send(): return lax.ppermute(value, 'blk', blk_flip(dza, dzb, dyl, dcore))]
    convert_element_type x3, other arithmetic: 5.09 us -> 0.61 us  [scatter_blk(): out = total(*(part[half:] for part in parts)).astype(BF16)]
    ppermute x15, waiting for transfers between devices: 35.2 us -> 31.6 us  [swap(): return lax.ppermute(value, 'dp', dp_flip(du, dv, ds))]
    pallas_call x2 -> x7, Pallas kernels: 17.8 us -> 14.5 us  [the longest x1 5.55 us: forward(): pl.pallas_call(body, in_specs=[SMEM, VMEM, VMEM] + [VMEM] * n, out_specs=...]
  transfers between devices with their start and end apart: 55 -> 55, of which waited for: 26 -> 27; matrix products, arithmetic and copies ran while one was open for 11% -> 3% of each run, Pallas kernels for 14% -> 17%
where the time goes in v1:
time: 196 us; the launch traced here: 193 us
  waiting for transfers between devices  90.1 us (46%)
  starting transfers between devices  53.8 us (27%)
  Pallas kernels  36.7 us (19%)
  local copies, waits for them, and re-layouts  6.7 us (3%)
  other arithmetic  5.09 us (3%)
    ppermute x40, waiting for transfers between devices, send(): return lax.ppermute(value, 'blk', blk_flip(dza, dzb, dyl, dcore))  58.5 us
    ppermute x15, waiting for transfers between devices, swap(): return lax.ppermute(value, 'dp', dp_flip(du, dv, ds))  31.6 us
    ppermute x40, starting transfers between devices, send(): return lax.ppermute(value, 'blk', blk_flip(dza, dzb, dyl, dcore))  27.9 us
    ppermute x15, starting transfers between devices, swap(): return lax.ppermute(value, 'dp', dp_flip(du, dv, ds))  25.9 us
    pallas_call x1, Pallas kernels, forward(): pl.pallas_call(body, in_specs=[SMEM, VMEM, VMEM] + [VMEM] * n, out_specs=...  5.55 us
    pallas_call x1, Pallas kernels, back(): pl.pallas_call(body, in_specs=[SMEM] + [VMEM] * 4, out_specs=[VMEM] * 2,...  5.42 us
    unnamed x24, local copies, waits for them, and re-layouts  5.36 us
    pallas_call x1, Pallas kernels, wgrad_y(): pl.pallas_call(body, in_specs=[SMEM, VMEM, VMEM], out_specs=[VMEM] * 2, o...  5.02 us
  transfers between devices with their start and end apart: 55, of which 27 were waited for; matrix products, arithmetic and copies ran while one was open for 3% of the time, Pallas kernels for 17%

profile of v1, /device:TPU:4, one launch (start us, length us, event | category | flops | bytes accessed | tf_op | source)
XLA Modules:
  0.0 193.3 jit_solution(7610926886413819408)
XLA Ops:
  2.3 3.9 %collective-permute-start.5 = (bf16[40,3072]{1,0:T(8,128)(2,1)}, bf16[40,3072]{1,0:T(8,128)(2,1)S(1)}, u32[]{:S(2)}, u32[]{:S(2)}) collective-permute-start(bf16[40,3072]{1,0:T(8,128)(2,1)} %refs_0_.5), channel_id=1, source_target_pairs={{0,8},{1,9},{2,10},{3,11},{4,12},{5,13},{6,14},{7,15},{8,0},{9,1},... | collective-permute-start | bytes 737288 | tf_op jit(solution)/shard_map/ppermute | solution.py:48
  10.2 3.0 %collective-permute-done.5.refs_6_ = bf16[40,3072]{1,0:T(8,128)(2,1)S(1)} collective-permute-done((bf16[40,3072]{1,0:T(8,128)(2,1)}, bf16[40,3072]{1,0:T(8,128)(2,1)S(1)}, u32[]{:S(2)}, u32[]{:S(2)}) %collective-permute-start.5) | collective-permute-done | bytes 245792 | tf_op jit(solution)/shard_map/ppermute | solution.py:48
  13.2 3.5 %collective-permute-start.20 = (bf16[40,3072]{1,0:T(8,128)(2,1)S(1)}, bf16[40,3072]{1,0:T(8,128)(2,1)S(1)}, u32[]{:S(2)}, u32[]{:S(2)}) collective-permute-start(bf16[40,3072]{1,0:T(8,128)(2,1)S(1)} %multiply_convert_fusion.1.refs_0_), channel_id=1, source_target_pairs={{0,8},{1,9},{2,10},{3,11},{4,12},{5,13},{6,14},{7,15},{8,0},{9,1},... | collective-permute-start | bytes 737288 | tf_op jit(solution)/shard_map/ppermute | solution.py:48
  16.7 2.8 %collective-permute-done.3.refs_4_ = bf16[40,3072]{1,0:T(8,128)(2,1)S(1)} collective-permute-done((bf16[40,3072]{1,0:T(8,128)(2,1)}, bf16[40,3072]{1,0:T(8,128)(2,1)S(1)}, u32[]{:S(2)}, u32[]{:S(2)}) %collective-permute-start.3) | collective-permute-done | bytes 245792 | tf_op jit(solution)/shard_map/ppermute | solution.py:48
  20.6 2.6 %collective-permute-start.2 = (bf16[40,3072]{1,0:T(8,128)(2,1)S(1)}, bf16[40,3072]{1,0:T(8,128)(2,1)S(1)}, u32[]{:S(2)}, u32[]{:S(2)}) collective-permute-start(bf16[40,3072]{1,0:T(8,128)(2,1)S(1)} %collective-permute-done.refs_1_), channel_id=1, source_target_pairs={{0,12},{1,13},{2,14},{3,15},{4,8},{5,9},{6,10},{7,11},{8,4},{9,5},... | collective-permute-start | bytes 737288 | tf_op jit(solution)/shard_map/ppermute | solution.py:48
  24.4 5.2 %collective-permute-done.16.refs_2_ = bf16[40,3072]{1,0:T(8,128)(2,1)S(1)} collective-permute-done((bf16[40,3072]{1,0:T(8,128)(2,1)S(1)}, bf16[40,3072]{1,0:T(8,128)(2,1)S(1)}, u32[]{:S(2)}, u32[]{:S(2)}) %collective-permute-start.16) | collective-permute-done | bytes 245792 | tf_op jit(solution)/shard_map/ppermute | solution.py:48
  30.6 2.6 %collective-permute-done.2.refs_3_ = bf16[40,3072]{1,0:T(8,128)(2,1)S(1)} collective-permute-done((bf16[40,3072]{1,0:T(8,128)(2,1)S(1)}, bf16[40,3072]{1,0:T(8,128)(2,1)S(1)}, u32[]{:S(2)}, u32[]{:S(2)}) %collective-permute-start.2) | collective-permute-done | bytes 245792 | tf_op jit(solution)/shard_map/ppermute | solution.py:48
  35.7 3.3 %collective-permute-start.17 = (bf16[40,3072]{1,0:T(8,128)(2,1)S(1)}, bf16[40,3072]{1,0:T(8,128)(2,1)S(1)}, u32[]{:S(2)}, u32[]{:S(2)}) collective-permute-start(bf16[40,3072]{1,0:T(8,128)(2,1)S(1)} %collective-permute-done.15.refs_1_), channel_id=1, source_target_pairs={{0,12},{1,13},{2,14},{3,15},{4,8},{5,9},{6,10},{7,11},{8,4},{9,5},... | collective-permute-start | bytes 737288 | tf_op jit(solution)/shard_map/ppermute | solution.py:48
  41.5 2.7 %collective-permute-done.17.refs_3_ = bf16[40,3072]{1,0:T(8,128)(2,1)S(1)} collective-permute-done((bf16[40,3072]{1,0:T(8,128)(2,1)S(1)}, bf16[40,3072]{1,0:T(8,128)(2,1)S(1)}, u32[]{:S(2)}, u32[]{:S(2)}) %collective-permute-start.17) | collective-permute-done | bytes 245792 | tf_op jit(solution)/shard_map/ppermute | solution.py:48
  44.2 2.3 %collective-permute-done.19.refs_5_ = bf16[40,3072]{1,0:T(8,128)(2,1)} collective-permute-done((bf16[40,3072]{1,0:T(8,128)(2,1)S(1)}, bf16[40,3072]{1,0:T(8,128)(2,1)}, u32[]{:S(2)}, u32[]{:S(2)}) %collective-permute-start.19) | collective-permute-done | bytes 245792 | tf_op jit(solution)/shard_map/ppermute | solution.py:48
  53.9 5.5 %shard_map.130 = (bf16[640,3072]{1,0:T(8,128)(2,1)S(1)}, bf16[640,512]{1,0:T(8,128)(2,1)S(1)}, f32[640,512]{1,0:T(8,128)S(1)}, f32[640,512]{1,0:T(8,128)S(1)}) custom-call(f32[3]{0:T(128)S(1)} %multiply_exponential_fusion.scales, bf16[3072,512]{1,0:T(8,128)(2,1)S(1)} %shard_map.128.w_gate, bf16[3072,512]{1,0:T(8,128)(2,1)S(1)} %shard_map.129.w_up, ...), custom_call_target="tpu_custom_call" | custom-call | flops 4026531840 | bytes 17432576 | tf_op jit(solution)/shard_map/pallas_call | solution.py:403
  59.5 4.2 %shard_map.131 = (bf16[640,3072]{1,0:T(8,128)(2,1)S(1)}, bf16[256,1536]{1,0:T(8,128)(2,1)S(1)}, bf16[256,1536]{1,0:T(8,128)(2,1)S(1)}, bf16[256,1536]{1,0:T(8,128)(2,1)S(1)}, bf16[256,1536]{1,0:T(8,128)(2,1)S(1)}) custom-call(s32[5]{0:T(128)S(1)} %dynamic-slice_bitcast_fusion.table, bf16[640,512]{1,0:T(8,128)(2,1)S(1)} %get-tuple-element.47.left.hidden, ...), custom_call_target="tpu_custom_call" | custom-call | flops 2013265920 | bytes 7733248 | tf_op jit(solution)/shard_map/pallas_call | solution.py:166
  65.0 2.8 %shard_map.133 = (bf16[640,512]{1,0:T(8,128)(2,1)S(1)}, bf16[640,512]{1,0:T(8,128)(2,1)S(1)}) custom-call(f32[3]{0:T(128)S(1)} %multiply_exponential_fusion.scales, bf16[640,3072]{1,0:T(8,128)(2,1)S(1)} %get-tuple-element.50.scaled, bf16[512,3072]{1,0:T(8,128)(2,1)S(1)} %copy-done, f32[640,512]{1,0:T(8,128)S(1)} %get-tuple-element.51.to_gate, ...), custom_call_target="tpu_custom_call" | custom-call | flops 2013265920 | bytes 11010048 | tf_op jit(solution)/shard_map/pallas_call | solution.py:434
  67.8 3.2 %shard_map.139 = (bf16[256,1536]{1,0:T(8,128)(2,1)S(1)}, bf16[256,1536]{1,0:T(8,128)(2,1)S(1)}, bf16[256,1536]{1,0:T(8,128)(2,1)S(1)}, bf16[256,1536]{1,0:T(8,128)(2,1)S(1)}) custom-call(s32[5]{0:T(128)S(1)} %dynamic-slice_bitcast_fusion.table, bf16[640,512]{1,0:T(8,128)(2,1)S(1)} %get-tuple-element.54.d_up.left, bf16[640,3072]{1,0:T(8,128)(2,1)S(1)} %get-tuple-element.60.right), custom_call_target="tpu_custom_call" | custom-call | flops 2013265920 | bytes 7733248 | tf_op jit(solution)/shard_map/pallas_call | solution.py:202
  74.6 5.0 %shard_map.136 = (bf16[512,1536]{1,0:T(8,128)(2,1)S(1)}, bf16[512,1536]{1,0:T(8,128)(2,1)S(1)}) custom-call(s32[5]{0:T(128)S(1)} %dynamic-slice_bitcast_fusion.table, bf16[640,512]{1,0:T(8,128)(2,1)S(1)} %get-tuple-element.53.d_gate.left, bf16[640,3072]{1,0:T(8,128)(2,1)S(1)} %get-tuple-element.60.right), custom_call_target="tpu_custom_call" | custom-call | flops 2013265920 | bytes 7733248 | tf_op jit(solution)/shard_map/pallas_call | solution.py:237
  79.6 3.0 %collective-permute-start.40 = (bf16[512,1536]{1,0:T(8,128)(2,1)S(1)}, bf16[512,1536]{1,0:T(8,128)(2,1)S(1)}, u32[]{:S(2)}, u32[]{:S(2)}) collective-permute-start(bf16[512,1536]{1,0:T(8,128)(2,1)S(1)} %get-tuple-element.62), channel_id=1, source_target_pairs={{0,16},{16,0},{32,48},{48,32},{64,80},{80,64},{96,112},{112,96},{1... | collective-permute-start | bytes 4718600 | tf_op jit(solution)/shard_map/ppermute | solution.py:52
  82.6 5.4 %shard_map.134 = (bf16[320,3072]{1,0:T(8,128)(2,1)S(1)}, bf16[320,3072]{1,0:T(8,128)(2,1)S(1)}) custom-call(f32[3]{0:T(128)S(1)} %multiply_exponential_fusion.scales, bf16[640,512]{1,0:T(8,128)(2,1)S(1)} %get-tuple-element.53.d_gate.left, bf16[640,512]{1,0:T(8,128)(2,1)S(1)} %get-tuple-element.54.d_up.left, bf16[3072,512]{1,0:T(8,128)(2,1)S(1)} %copy-done.2, ...), custom_call_target="tpu_custom_call" | custom-call | flops 4026531840 | bytes 11534336 | tf_op jit(solution)/shard_map/pallas_call | solution.py:487
  88.1 2.5 %shard_map.132 = (bf16[320,3072]{1,0:T(8,128)(2,1)S(1)}, bf16[320,3072]{1,0:T(8,128)(2,1)S(1)}) custom-call(bf16[640,512]{1,0:T(8,128)(2,1)S(1)} %get-tuple-element.47.left.hidden, bf16[512,3072]{1,0:T(8,128)(2,1)S(1)} %copy-done), custom_call_target="tpu_custom_call" | custom-call | flops 2013265920 | bytes 8257536 | tf_op jit(solution)/shard_map/pallas_call | solution.py:461
  91.4 8.9 %collective-permute-done.45.got_a = bf16[256,1536]{1,0:T(8,128)(2,1)S(1)} collective-permute-done((bf16[256,1536]{1,0:T(8,128)(2,1)S(1)}, bf16[256,1536]{1,0:T(8,128)(2,1)S(1)}, u32[]{:S(2)}, u32[]{:S(2)}) %collective-permute-start.45) | collective-permute-done | bytes 786464 | tf_op jit(solution)/shard_map/ppermute | solution.py:52
  103.5 7.3 %collective-permute-done.52.two_a = bf16[256,768]{1,0:T(8,128)(2,1)S(1)} collective-permute-done((bf16[256,768]{1,0:T(8,128)(2,1)S(1)}, bf16[256,768]{1,0:T(8,128)(2,1)S(1)}, u32[]{:S(2)}, u32[]{:S(2)}) %collective-permute-start.52) | collective-permute-done | bytes 393248 | tf_op jit(solution)/shard_map/ppermute | solution.py:52
  114.7 5.7 %collective-permute-done.47.two_a = bf16[256,768]{1,0:T(8,128)(2,1)S(1)} collective-permute-done((bf16[256,768]{1,0:T(8,128)(2,1)S(1)}, bf16[256,768]{1,0:T(8,128)(2,1)S(1)}, u32[]{:S(2)}, u32[]{:S(2)}) %collective-permute-start.47) | collective-permute-done | bytes 393248 | tf_op jit(solution)/shard_map/ppermute | solution.py:52
  120.4 2.9 %collective-permute-start.54 = (bf16[512,384]{1,0:T(8,128)(2,1)S(1)}, bf16[512,384]{1,0:T(8,128)(2,1)S(1)}, u32[]{:S(2)}, u32[]{:S(2)}) collective-permute-start(bf16[512,384]{1,0:T(8,128)(2,1)S(1)} %get-tuple-element.82), channel_id=1, source_target_pairs={{0,16},{16,0},{32,48},{48,32},{64,80},{80,64},{96,112},{112,96},{1... | collective-permute-start | bytes 1179656 | tf_op jit(solution)/shard_map/ppermute | solution.py:52
  125.7 2.2 %collective-permute-start.43 = (bf16[256,768]{1,0:T(8,128)(2,1)S(1)}, bf16[256,768]{1,0:T(8,128)(2,1)S(1)}, u32[]{:S(2)}, u32[]{:S(2)}) collective-permute-start(bf16[256,768]{1,0:T(8,128)(2,1)S(1)} %get-tuple-element.66), channel_id=1, source_target_pairs={{0,96},{16,112},{32,64},{48,80},{64,32},{80,48},{96,0},{112,16},{1... | collective-permute-start | bytes 1179656 | tf_op jit(solution)/shard_map/ppermute | solution.py:52
  127.8 6.0 %collective-permute-done.54.refs_1_ = bf16[512,384]{1,0:T(8,128)(2,1)S(1)} collective-permute-done((bf16[512,384]{1,0:T(8,128)(2,1)S(1)}, bf16[512,384]{1,0:T(8,128)(2,1)S(1)}, u32[]{:S(2)}, u32[]{:S(2)}) %collective-permute-start.54) | collective-permute-done | bytes 393248 | tf_op jit(solution)/shard_map/ppermute | solution.py:52
  133.8 3.6 %collective-permute-start.41 = (bf16[256,768]{1,0:T(8,128)(2,1)S(1)}, bf16[256,768]{1,0:T(8,128)(2,1)S(1)}, u32[]{:S(2)}, u32[]{:S(2)}) collective-permute-start(bf16[256,768]{1,0:T(8,128)(2,1)S(1)} %get-tuple-element.64), channel_id=1, source_target_pairs={{0,32},{16,48},{32,0},{48,16},{64,96},{80,112},{96,64},{112,80},{1... | collective-permute-start | bytes 1179656 | tf_op jit(solution)/shard_map/ppermute | solution.py:52
  141.0 3.2 %collective-permute-start.44 = (bf16[256,384]{1,0:T(8,128)(2,1)S(1)}, bf16[256,384]{1,0:T(8,128)(2,1)S(1)}, u32[]{:S(2)}, u32[]{:S(2)}) collective-permute-start(bf16[256,384]{1,0:T(8,128)(2,1)S(1)} %add_convert_fusion.7), channel_id=1, source_target_pairs={{0,32},{16,48},{32,0},{48,16},{64,96},{80,112},{96,64},{112,80},{1... | collective-permute-start | bytes 589832 | tf_op jit(solution)/shard_map/ppermute | solution.py:52
  147.8 2.5 %collective-permute-done.42.refs_2_ = bf16[256,384]{1,0:T(8,128)(2,1)S(1)} collective-permute-done((bf16[256,384]{1,0:T(8,128)(2,1)S(1)}, bf16[256,384]{1,0:T(8,128)(2,1)S(1)}, u32[]{:S(2)}, u32[]{:S(2)}) %collective-permute-start.42) | collective-permute-done | bytes 196640 | tf_op jit(solution)/shard_map/ppermute | solution.py:52
  151.8 2.2 %collective-permute-done.35 = bf16[40,3072]{1,0:T(8,128)(2,1)S(1)} collective-permute-done((bf16[40,3072]{1,0:T(8,128)(2,1)S(1)}, bf16[40,3072]{1,0:T(8,128)(2,1)S(1)}, u32[]{:S(2)}, u32[]{:S(2)}) %collective-permute-start.35) | collective-permute-done | bytes 245792 | tf_op jit(solution)/shard_map/ppermute | solution.py:48
  156.2 18.9 %collective-permute-done.31 = bf16[160,3072]{1,0:T(8,128)(2,1)S(1)} collective-permute-done((bf16[160,3072]{1,0:T(8,128)(2,1)S(1)}, bf16[160,3072]{1,0:T(8,128)(2,1)S(1)}, u32[]{:S(2)}, u32[]{:S(2)}) %collective-permute-start.31) | collective-permute-done | bytes 983072 | tf_op jit(solution)/shard_map/ppermute | solution.py:48
  175.9 5.0 %collective-permute-done.38 = bf16[80,3072]{1,0:T(8,128)(2,1)S(1)} collective-permute-done((bf16[80,3072]{1,0:T(8,128)(2,1)S(1)}, bf16[80,3072]{1,0:T(8,128)(2,1)S(1)}, u32[]{:S(2)}, u32[]{:S(2)}) %collective-permute-start.38) | collective-permute-done | bytes 491552 | tf_op jit(solution)/shard_map/ppermute | solution.py:48
  181.5 3.9 %collective-permute-done.32 = bf16[80,3072]{1,0:T(8,128)(2,1)S(1)} collective-permute-done((bf16[80,3072]{1,0:T(8,128)(2,1)S(1)}, bf16[80,3072]{1,0:T(8,128)(2,1)S(1)}, u32[]{:S(2)}, u32[]{:S(2)}) %collective-permute-start.32) | collective-permute-done | bytes 491552 | tf_op jit(solution)/shard_map/ppermute | solution.py:48
  188.1 3.7 %collective-permute-done.33 = bf16[40,3072]{1,0:T(8,128)(2,1)S(1)} collective-permute-done((bf16[40,3072]{1,0:T(8,128)(2,1)S(1)}, bf16[40,3072]{1,0:T(8,128)(2,1)S(1)}, u32[]{:S(2)}, u32[]{:S(2)}) %collective-permute-start.33) | collective-permute-done | bytes 245792 | tf_op jit(solution)/shard_map/ppermute | solution.py:48
  (137 shorter events, 52.7 us)
Async XLA Ops:
  2.3 10.9 %collective-permute-start.5 = (bf16[40,3072]{1,0:T(8,128)(2,1)}, bf16[40,3072]{1,0:T(8,128)(2,1)S(1)}, u32[]{:S(2)}, u32[]{:S(2)}) collective-permute-start(bf16[40,3072]{1,0:T(8,128)(2,1)} %refs_0_.5), channel_id=1, source_target_pairs={{0,8},{1,9},{2,10},{3,11},{4,12},{5,13},{6,14},{7,15},{8,0},{9,1},... | collective-permute-start | bytes 737288 | tf_op jit(solution)/shard_map/ppermute | solution.py:48
  6.2 13.3 %collective-permute-start.3 = (bf16[40,3072]{1,0:T(8,128)(2,1)}, bf16[40,3072]{1,0:T(8,128)(2,1)S(1)}, u32[]{:S(2)}, u32[]{:S(2)}) collective-permute-start(bf16[40,3072]{1,0:T(8,128)(2,1)} %refs_0_.5), channel_id=1, source_target_pairs={{0,4},{1,5},{2,6},{3,7},{4,0},{5,1},{6,2},{7,3},{8,12},{9,13},{10,... | collective-permute-start | bytes 737288 | tf_op jit(solution)/shard_map/ppermute | solution.py:48
  7.2 12.3 %collective-permute-start.1 = (bf16[40,3072]{1,0:T(8,128)(2,1)}, bf16[40,3072]{1,0:T(8,128)(2,1)S(1)}, u32[]{:S(2)}, u32[]{:S(2)}) collective-permute-start(bf16[40,3072]{1,0:T(8,128)(2,1)} %refs_0_.5), channel_id=1, source_target_pairs={{0,12},{1,13},{2,14},{3,15},{4,8},{5,9},{6,10},{7,11},{8,4},{9,5},... | collective-permute-start | bytes 737288 | tf_op jit(solution)/shard_map/ppermute | solution.py:48
  7.2 13.4 %collective-permute-start.7 = (bf16[40,3072]{1,0:T(8,128)(2,1)}, bf16[40,3072]{1,0:T(8,128)(2,1)S(1)}, u32[]{:S(2)}, u32[]{:S(2)}) collective-permute-start(bf16[40,3072]{1,0:T(8,128)(2,1)} %refs_0_.5), channel_id=1, source_target_pairs={{0,1},{1,0},{2,3},{3,2},{4,5},{5,4},{6,7},{7,6},{8,9},{9,8},{10,11... | collective-permute-start | bytes 737288 | tf_op jit(solution)/shard_map/ppermute | solution.py:48
  9.0 11.7 %collective-permute-start.15 = (bf16[40,3072]{1,0:T(8,128)(2,1)S(1)}, bf16[40,3072]{1,0:T(8,128)(2,1)S(1)}, u32[]{:S(2)}, u32[]{:S(2)}) collective-permute-start(bf16[40,3072]{1,0:T(8,128)(2,1)S(1)} %multiply_convert_fusion.1.refs_0_), channel_id=1, source_target_pairs={{0,2},{1,3},{2,0},{3,1},{4,6},{5,7},{6,4},{7,5},{8,10},{9,11},{10,... | collective-permute-start | bytes 737288 | tf_op jit(solution)/shard_map/ppermute | solution.py:48
  13.2 10.1 %collective-permute-start.20 = (bf16[40,3072]{1,0:T(8,128)(2,1)S(1)}, bf16[40,3072]{1,0:T(8,128)(2,1)S(1)}, u32[]{:S(2)}, u32[]{:S(2)}) collective-permute-start(bf16[40,3072]{1,0:T(8,128)(2,1)S(1)} %multiply_convert_fusion.1.refs_0_), channel_id=1, source_target_pairs={{0,8},{1,9},{2,10},{3,11},{4,12},{5,13},{6,14},{7,15},{8,0},{9,1},... | collective-permute-start | bytes 737288 | tf_op jit(solution)/shard_map/ppermute | solution.py:48
  19.5 10.0 %collective-permute-start.16 = (bf16[40,3072]{1,0:T(8,128)(2,1)S(1)}, bf16[40,3072]{1,0:T(8,128)(2,1)S(1)}, u32[]{:S(2)}, u32[]{:S(2)}) collective-permute-start(bf16[40,3072]{1,0:T(8,128)(2,1)S(1)} %multiply_convert_fusion.1.refs_0_), channel_id=1, source_target_pairs={{0,12},{1,13},{2,14},{3,15},{4,8},{5,9},{6,10},{7,11},{8,4},{9,5},... | collective-permute-start | bytes 737288 | tf_op jit(solution)/shard_map/ppermute | solution.py:48
  19.5 10.6 %collective-permute-start.18 = (bf16[40,3072]{1,0:T(8,128)(2,1)S(1)}, bf16[40,3072]{1,0:T(8,128)(2,1)S(1)}, u32[]{:S(2)}, u32[]{:S(2)}) collective-permute-start(bf16[40,3072]{1,0:T(8,128)(2,1)S(1)} %multiply_convert_fusion.1.refs_0_), channel_id=1, source_target_pairs={{0,4},{1,5},{2,6},{3,7},{4,0},{5,1},{6,2},{7,3},{8,12},{9,13},{10,... | collective-permute-start | bytes 737288 | tf_op jit(solution)/shard_map/ppermute | solution.py:48
  20.6 12.5 %collective-permute-start.2 = (bf16[40,3072]{1,0:T(8,128)(2,1)S(1)}, bf16[40,3072]{1,0:T(8,128)(2,1)S(1)}, u32[]{:S(2)}, u32[]{:S(2)}) collective-permute-start(bf16[40,3072]{1,0:T(8,128)(2,1)S(1)} %collective-permute-done.refs_1_), channel_id=1, source_target_pairs={{0,12},{1,13},{2,14},{3,15},{4,8},{5,9},{6,10},{7,11},{8,4},{9,5},... | collective-permute-start | bytes 737288 | tf_op jit(solution)/shard_map/ppermute | solution.py:48
  23.3 10.6 %collective-permute-start.4 = (bf16[40,3072]{1,0:T(8,128)(2,1)S(1)}, bf16[40,3072]{1,0:T(8,128)(2,1)S(1)}, u32[]{:S(2)}, u32[]{:S(2)}) collective-permute-start(bf16[40,3072]{1,0:T(8,128)(2,1)S(1)} %collective-permute-done.refs_1_), channel_id=1, source_target_pairs={{0,4},{1,5},{2,6},{3,7},{4,0},{5,1},{6,2},{7,3},{8,12},{9,13},{10,... | collective-permute-start | bytes 737288 | tf_op jit(solution)/shard_map/ppermute | solution.py:48
  30.1 9.7 %collective-permute-start.13 = (bf16[40,3072]{1,0:T(8,128)(2,1)S(1)}, bf16[40,3072]{1,0:T(8,128)(2,1)S(1)}, u32[]{:S(2)}, u32[]{:S(2)}) collective-permute-start(bf16[40,3072]{1,0:T(8,128)(2,1)S(1)} %collective-permute-done.5.refs_6_), channel_id=1, source_target_pairs={{0,1},{1,0},{2,3},{3,2},{4,5},{5,4},{6,7},{7,6},{8,9},{9,8},{10,11... | collective-permute-start | bytes 737288 | tf_op jit(solution)/shard_map/ppermute | solution.py:48
  40.9 11.4 %collective-permute-start.23 = (bf16[40,3072]{1,0:T(8,128)(2,1)S(1)}, bf16[40,3072]{1,0:T(8,128)(2,1)S(1)}, u32[]{:S(2)}, u32[]{:S(2)}) collective-permute-start(bf16[40,3072]{1,0:T(8,128)(2,1)S(1)} %collective-permute-done.15.refs_1_), channel_id=1, source_target_pairs={{0,1},{1,0},{2,3},{3,2},{4,5},{5,4},{6,7},{7,6},{8,9},{9,8},{10,11... | collective-permute-start | bytes 737288 | tf_op jit(solution)/shard_map/ppermute | solution.py:48
  41.0 11.9 %collective-permute-start.28 = (bf16[40,3072]{1,0:T(8,128)(2,1)S(1)}, bf16[40,3072]{1,0:T(8,128)(2,1)S(1)}, u32[]{:S(2)}, u32[]{:S(2)}) collective-permute-start(bf16[40,3072]{1,0:T(8,128)(2,1)S(1)} %collective-permute-done.20.refs_6_), channel_id=1, source_target_pairs={{0,1},{1,0},{2,3},{3,2},{4,5},{5,4},{6,7},{7,6},{8,9},{9,8},{10,11... | collective-permute-start | bytes 737288 | tf_op jit(solution)/shard_map/ppermute | solution.py:48
  63.7 24.3 %collective-permute-start.50 = (bf16[256,1536]{1,0:T(8,128)(2,1)S(1)}, bf16[256,1536]{1,0:T(8,128)(2,1)S(1)}, u32[]{:S(2)}, u32[]{:S(2)}) collective-permute-start(bf16[256,1536]{1,0:T(8,128)(2,1)S(1)} %get-tuple-element.76), channel_id=1, source_target_pairs={{0,32},{16,48},{32,0},{48,16},{64,96},{80,112},{96,64},{112,80},{1... | collective-permute-start | bytes 2359304 | tf_op jit(solution)/shard_map/ppermute | solution.py:52
  65.0 25.7 %collective-permute-start.51 = (bf16[256,1536]{1,0:T(8,128)(2,1)S(1)}, bf16[256,1536]{1,0:T(8,128)(2,1)S(1)}, u32[]{:S(2)}, u32[]{:S(2)}) collective-permute-start(bf16[256,1536]{1,0:T(8,128)(2,1)S(1)} %get-tuple-element.78), channel_id=1, source_target_pairs={{0,96},{16,112},{32,64},{48,80},{64,32},{80,48},{96,0},{112,16},{1... | collective-permute-start | bytes 2359304 | tf_op jit(solution)/shard_map/ppermute | solution.py:52
  71.0 29.3 %collective-permute-start.45 = (bf16[256,1536]{1,0:T(8,128)(2,1)S(1)}, bf16[256,1536]{1,0:T(8,128)(2,1)S(1)}, u32[]{:S(2)}, u32[]{:S(2)}) collective-permute-start(bf16[256,1536]{1,0:T(8,128)(2,1)S(1)} %get-tuple-element.68), channel_id=1, source_target_pairs={{0,32},{16,48},{32,0},{48,16},{64,96},{80,112},{96,64},{112,80},{1... | collective-permute-start | bytes 2359304 | tf_op jit(solution)/shard_map/ppermute | solution.py:52
  73.1 28.2 %collective-permute-start.46 = (bf16[256,1536]{1,0:T(8,128)(2,1)S(1)}, bf16[256,1536]{1,0:T(8,128)(2,1)S(1)}, u32[]{:S(2)}, u32[]{:S(2)}) collective-permute-start(bf16[256,1536]{1,0:T(8,128)(2,1)S(1)} %get-tuple-element.70), channel_id=1, source_target_pairs={{0,96},{16,112},{32,64},{48,80},{64,32},{80,48},{96,0},{112,16},{1... | collective-permute-start | bytes 2359304 | tf_op jit(solution)/shard_map/ppermute | solution.py:52
  79.6 45.7 %collective-permute-start.40 = (bf16[512,1536]{1,0:T(8,128)(2,1)S(1)}, bf16[512,1536]{1,0:T(8,128)(2,1)S(1)}, u32[]{:S(2)}, u32[]{:S(2)}) collective-permute-start(bf16[512,1536]{1,0:T(8,128)(2,1)S(1)} %get-tuple-element.62), channel_id=1, source_target_pairs={{0,16},{16,0},{32,48},{48,32},{64,80},{80,64},{96,112},{112,96},{1... | collective-permute-start | bytes 4718600 | tf_op jit(solution)/shard_map/ppermute | solution.py:52
  88.0 56.7 %collective-permute-start.34 = (bf16[320,3072]{1,0:T(8,128)(2,1)S(1)}, bf16[320,3072]{1,0:T(8,128)(2,1)S(1)}, u32[]{:S(2)}, u32[]{:S(2)}) collective-permute-start(bf16[320,3072]{1,0:T(8,128)(2,1)S(1)} %get-tuple-element.56), channel_id=1, source_target_pairs={{0,1},{1,0},{2,3},{3,2},{4,5},{5,4},{6,7},{7,6},{8,9},{9,8},{10,11... | collective-permute-start | bytes 5898248 | tf_op jit(solution)/shard_map/ppermute | solution.py:48
  90.7 56.6 %collective-permute-start.30 = (bf16[320,3072]{1,0:T(8,128)(2,1)S(1)}, bf16[320,3072]{1,0:T(8,128)(2,1)S(1)}, u32[]{:S(2)}, u32[]{:S(2)}) collective-permute-start(bf16[320,3072]{1,0:T(8,128)(2,1)S(1)} %get-tuple-element.49), channel_id=1, source_target_pairs={{0,1},{1,0},{2,3},{3,2},{4,5},{5,4},{6,7},{7,6},{8,9},{9,8},{10,11... | collective-permute-start | bytes 5898248 | tf_op jit(solution)/shard_map/ppermute | solution.py:48
  100.4 10.4 %collective-permute-start.52 = (bf16[256,768]{1,0:T(8,128)(2,1)S(1)}, bf16[256,768]{1,0:T(8,128)(2,1)S(1)}, u32[]{:S(2)}, u32[]{:S(2)}) collective-permute-start(bf16[256,768]{1,0:T(8,128)(2,1)S(1)} %get-tuple-element.79), channel_id=1, source_target_pairs={{0,96},{16,112},{32,64},{48,80},{64,32},{80,48},{96,0},{112,16},{1... | collective-permute-start | bytes 1179656 | tf_op jit(solution)/shard_map/ppermute | solution.py:52
  101.3 10.5 %collective-permute-start.53 = (bf16[256,768]{1,0:T(8,128)(2,1)S(1)}, bf16[256,768]{1,0:T(8,128)(2,1)S(1)}, u32[]{:S(2)}, u32[]{:S(2)}) collective-permute-start(bf16[256,768]{1,0:T(8,128)(2,1)S(1)} %get-tuple-element.80), channel_id=1, source_target_pairs={{0,32},{16,48},{32,0},{48,16},{64,96},{80,112},{96,64},{112,80},{1... | collective-permute-start | bytes 1179656 | tf_op jit(solution)/shard_map/ppermute | solution.py:52
  110.8 9.6 %collective-permute-start.47 = (bf16[256,768]{1,0:T(8,128)(2,1)S(1)}, bf16[256,768]{1,0:T(8,128)(2,1)S(1)}, u32[]{:S(2)}, u32[]{:S(2)}) collective-permute-start(bf16[256,768]{1,0:T(8,128)(2,1)S(1)} %get-tuple-element.71), channel_id=1, source_target_pairs={{0,96},{16,112},{32,64},{48,80},{64,32},{80,48},{96,0},{112,16},{1... | collective-permute-start | bytes 1179656 | tf_op jit(solution)/shard_map/ppermute | solution.py:52
  111.7 11.6 %collective-permute-start.48 = (bf16[256,768]{1,0:T(8,128)(2,1)S(1)}, bf16[256,768]{1,0:T(8,128)(2,1)S(1)}, u32[]{:S(2)}, u32[]{:S(2)}) collective-permute-start(bf16[256,768]{1,0:T(8,128)(2,1)S(1)} %get-tuple-element.72), channel_id=1, source_target_pairs={{0,32},{16,48},{32,0},{48,16},{64,96},{80,112},{96,64},{112,80},{1... | collective-permute-start | bytes 1179656 | tf_op jit(solution)/shard_map/ppermute | solution.py:52
  120.4 13.5 %collective-permute-start.54 = (bf16[512,384]{1,0:T(8,128)(2,1)S(1)}, bf16[512,384]{1,0:T(8,128)(2,1)S(1)}, u32[]{:S(2)}, u32[]{:S(2)}) collective-permute-start(bf16[512,384]{1,0:T(8,128)(2,1)S(1)} %get-tuple-element.82), channel_id=1, source_target_pairs={{0,16},{16,0},{32,48},{48,32},{64,80},{80,64},{96,112},{112,96},{1... | collective-permute-start | bytes 1179656 | tf_op jit(solution)/shard_map/ppermute | solution.py:52
  124.3 15.2 %collective-permute-start.49 = (bf16[512,384]{1,0:T(8,128)(2,1)S(1)}, bf16[512,384]{1,0:T(8,128)(2,1)S(1)}, u32[]{:S(2)}, u32[]{:S(2)}) collective-permute-start(bf16[512,384]{1,0:T(8,128)(2,1)S(1)} %get-tuple-element.74), channel_id=1, source_target_pairs={{0,16},{16,0},{32,48},{48,32},{64,80},{80,64},{96,112},{112,96},{1... | collective-permute-start | bytes 1179656 | tf_op jit(solution)/shard_map/ppermute | solution.py:52
  125.7 15.2 %collective-permute-start.43 = (bf16[256,768]{1,0:T(8,128)(2,1)S(1)}, bf16[256,768]{1,0:T(8,128)(2,1)S(1)}, u32[]{:S(2)}, u32[]{:S(2)}) collective-permute-start(bf16[256,768]{1,0:T(8,128)(2,1)S(1)} %get-tuple-element.66), channel_id=1, source_target_pairs={{0,96},{16,112},{32,64},{48,80},{64,32},{80,48},{96,0},{112,16},{1... | collective-permute-start | bytes 1179656 | tf_op jit(solution)/shard_map/ppermute | solution.py:52
  133.8 10.7 %collective-permute-start.41 = (bf16[256,768]{1,0:T(8,128)(2,1)S(1)}, bf16[256,768]{1,0:T(8,128)(2,1)S(1)}, u32[]{:S(2)}, u32[]{:S(2)}) collective-permute-start(bf16[256,768]{1,0:T(8,128)(2,1)S(1)} %get-tuple-element.64), channel_id=1, source_target_pairs={{0,32},{16,48},{32,0},{48,16},{64,96},{80,112},{96,64},{112,80},{1... | collective-permute-start | bytes 1179656 | tf_op jit(solution)/shard_map/ppermute | solution.py:52
  147.6 27.5 %collective-permute-start.31 = (bf16[160,3072]{1,0:T(8,128)(2,1)S(1)}, bf16[160,3072]{1,0:T(8,128)(2,1)S(1)}, u32[]{:S(2)}, u32[]{:S(2)}) collective-permute-start(bf16[160,3072]{1,0:T(8,128)(2,1)S(1)} %add_convert_fusion), channel_id=1, source_target_pairs={{0,4},{1,5},{2,6},{3,7},{4,0},{5,1},{6,2},{7,3},{8,12},{9,13},{10,... | collective-permute-start | bytes 2949128 | tf_op jit(solution)/shard_map/ppermute | solution.py:48
  155.7 20.2 %collective-permute-start.36 = (bf16[80,3072]{1,0:T(8,128)(2,1)S(1)}, bf16[80,3072]{1,0:T(8,128)(2,1)S(1)}, u32[]{:S(2)}, u32[]{:S(2)}) collective-permute-start(bf16[80,3072]{1,0:T(8,128)(2,1)S(1)} %pad_maximum_fusion), channel_id=1, source_target_pairs={{0,12},{1,13},{2,14},{3,15},{4,8},{5,9},{6,10},{7,11},{8,4},{9,5},... | collective-permute-start | bytes 1474568 | tf_op jit(solution)/shard_map/ppermute | solution.py:48
  156.0 24.9 %collective-permute-start.38 = (bf16[80,3072]{1,0:T(8,128)(2,1)S(1)}, bf16[80,3072]{1,0:T(8,128)(2,1)S(1)}, u32[]{:S(2)}, u32[]{:S(2)}) collective-permute-start(bf16[80,3072]{1,0:T(8,128)(2,1)S(1)} %pad_maximum_fusion.1), channel_id=1, source_target_pairs={{0,4},{1,5},{2,6},{3,7},{4,0},{5,1},{6,2},{7,3},{8,12},{9,13},{10,... | collective-permute-start | bytes 1474568 | tf_op jit(solution)/shard_map/ppermute | solution.py:48
  175.3 10.1 %collective-permute-start.32 = (bf16[80,3072]{1,0:T(8,128)(2,1)S(1)}, bf16[80,3072]{1,0:T(8,128)(2,1)S(1)}, u32[]{:S(2)}, u32[]{:S(2)}) collective-permute-start(bf16[80,3072]{1,0:T(8,128)(2,1)S(1)} %add_convert_fusion.1), channel_id=1, source_target_pairs={{0,12},{1,13},{2,14},{3,15},{4,8},{5,9},{6,10},{7,11},{8,4},{9,5},... | collective-permute-start | bytes 1474568 | tf_op jit(solution)/shard_map/ppermute | solution.py:48
  (35 other events, 199.2 us)

commit v2 on v1

--- a/solution.py
+++ b/solution.py
@@ -68,15 +68,6 @@
     return sum(part.astype(F32) for part in parts)
 
 
-def scatter_blk(own, other):
-    parts = [own, send(other, dcore=1)]
-    for flip in ({"dza": 1}, {"dzb": 1}, {"dyl": 1}):
-        half = parts[0].shape[0] // 2
-        out = total(*(part[half:] for part in parts)).astype(BF16)
-        parts = [part[:half] for part in parts] + [send(out, **flip)]
-    return total(*parts)
-
-
 def merge_rows(own, got):
     rows, d = own.shape
     n = rows // 8
@@ -98,7 +89,7 @@
     )(own, got)
 
 
-def scatter_blk_both(own, other):
+def scatter_blk(own, other):
     got = send(other, dcore=1)
     n = own.shape[0] // 8
     near, far_a, far_b = merge_rows(own, got)
@@ -525,7 +516,7 @@
     expert_out = scatter_blk(own, other) * scales[2]
     mixed = (combine_later * expert_out).astype(BF16)
     other, own = back(scales, d_gate, d_up, w_gate, w_up)
-    input_grad = scatter_blk_both(own, other)
+    input_grad = scatter_blk(own, other)
     return (
         mixed,
         input_grad.astype(BF16),

time: 196 us -> 187 us (0.954)
  waiting for transfers between devices: 90.1 us -> 82.2 us
    ppermute x40 -> x42, waiting for transfers between devices: 58.5 us -> 52.6 us  [send(): return lax.ppermute(value, 'blk', blk_flip(dza, dzb, dyl, dcore))]
    ppermute x15, starting transfers between devices: 25.9 us -> 23.7 us  [swap(): return lax.ppermute(value, 'dp', dp_flip(du, dv, ds))]
    ppermute x40 -> x42, starting transfers between devices: 27.9 us -> 30 us  [send(): return lax.ppermute(value, 'blk', blk_flip(dza, dzb, dyl, dcore))]
    ppermute x15, waiting for transfers between devices: 31.6 us -> 29.6 us  [swap(): return lax.ppermute(value, 'dp', dp_flip(du, dv, ds))]
  transfers between devices with their start and end apart: 55 -> 57, of which waited for: 27 -> 26; matrix products, arithmetic and copies ran while one was open for 3% -> 3% of each run, Pallas kernels for 17% -> 18%
where the time goes in v2:
time: 187 us; the launch traced here: 186 us
  waiting for transfers between devices  82.2 us (44%)
  starting transfers between devices  53.7 us (29%)
  Pallas kernels  37.1 us (20%)
  local copies, waits for them, and re-layouts  6.76 us (4%)
  other arithmetic  4.74 us (3%)
    ppermute x42, waiting for transfers between devices, send(): return lax.ppermute(value, 'blk', blk_flip(dza, dzb, dyl, dcore))  52.6 us
    ppermute x42, starting transfers between devices, send(): return lax.ppermute(value, 'blk', blk_flip(dza, dzb, dyl, dcore))  30 us
    ppermute x15, waiting for transfers between devices, swap(): return lax.ppermute(value, 'dp', dp_flip(du, dv, ds))  29.6 us
    ppermute x15, starting transfers between devices, swap(): return lax.ppermute(value, 'dp', dp_flip(du, dv, ds))  23.7 us
    pallas_call x1, Pallas kernels, forward(): pl.pallas_call(body, in_specs=[SMEM, VMEM, VMEM] + [VMEM] * n, out_specs=...  5.53 us
    pallas_call x1, Pallas kernels, back(): pl.pallas_call(body, in_specs=[SMEM] + [VMEM] * 4, out_specs=[VMEM] * 2,...  5.42 us
    unnamed x24, local copies, waits for them, and re-layouts  5.36 us
    pallas_call x1, Pallas kernels, wgrad_y(): pl.pallas_call(body, in_specs=[SMEM, VMEM, VMEM], out_specs=[VMEM] * 2, o...  5.03 us
  transfers between devices with their start and end apart: 57, of which 26 were waited for; matrix products, arithmetic and copies ran while one was open for 3% of the time, Pallas kernels for 18%

profile of v2, /device:TPU:4, one launch (start us, length us, event | category | flops | bytes accessed | tf_op | source)
XLA Modules:
  0.0 185.5 jit_solution(12585260005295179023)
XLA Ops:
  2.3 3.9 %collective-permute-start.5 = (bf16[40,3072]{1,0:T(8,128)(2,1)}, bf16[40,3072]{1,0:T(8,128)(2,1)S(1)}, u32[]{:S(2)}, u32[]{:S(2)}) collective-permute-start(bf16[40,3072]{1,0:T(8,128)(2,1)} %refs_0_.5), channel_id=1, source_target_pairs={{0,8},{1,9},{2,10},{3,11},{4,12},{5,13},{6,14},{7,15},{8,0},{9,1},... | collective-permute-start | bytes 737288 | tf_op jit(solution)/shard_map/ppermute | solution.py:48
  10.2 3.0 %collective-permute-done.5.refs_6_ = bf16[40,3072]{1,0:T(8,128)(2,1)S(1)} collective-permute-done((bf16[40,3072]{1,0:T(8,128)(2,1)}, bf16[40,3072]{1,0:T(8,128)(2,1)S(1)}, u32[]{:S(2)}, u32[]{:S(2)}) %collective-permute-start.5) | collective-permute-done | bytes 245792 | tf_op jit(solution)/shard_map/ppermute | solution.py:48
  13.2 3.5 %collective-permute-start.20 = (bf16[40,3072]{1,0:T(8,128)(2,1)S(1)}, bf16[40,3072]{1,0:T(8,128)(2,1)S(1)}, u32[]{:S(2)}, u32[]{:S(2)}) collective-permute-start(bf16[40,3072]{1,0:T(8,128)(2,1)S(1)} %multiply_convert_fusion.1.refs_0_), channel_id=1, source_target_pairs={{0,8},{1,9},{2,10},{3,11},{4,12},{5,13},{6,14},{7,15},{8,0},{9,1},... | collective-permute-start | bytes 737288 | tf_op jit(solution)/shard_map/ppermute | solution.py:48
  16.7 2.8 %collective-permute-done.3.refs_4_ = bf16[40,3072]{1,0:T(8,128)(2,1)S(1)} collective-permute-done((bf16[40,3072]{1,0:T(8,128)(2,1)}, bf16[40,3072]{1,0:T(8,128)(2,1)S(1)}, u32[]{:S(2)}, u32[]{:S(2)}) %collective-permute-start.3) | collective-permute-done | bytes 245792 | tf_op jit(solution)/shard_map/ppermute | solution.py:48
  20.6 2.6 %collective-permute-start.2 = (bf16[40,3072]{1,0:T(8,128)(2,1)S(1)}, bf16[40,3072]{1,0:T(8,128)(2,1)S(1)}, u32[]{:S(2)}, u32[]{:S(2)}) collective-permute-start(bf16[40,3072]{1,0:T(8,128)(2,1)S(1)} %collective-permute-done.refs_1_), channel_id=1, source_target_pairs={{0,12},{1,13},{2,14},{3,15},{4,8},{5,9},{6,10},{7,11},{8,4},{9,5},... | collective-permute-start | bytes 737288 | tf_op jit(solution)/shard_map/ppermute | solution.py:48
  24.4 5.2 %collective-permute-done.16.refs_2_ = bf16[40,3072]{1,0:T(8,128)(2,1)S(1)} collective-permute-done((bf16[40,3072]{1,0:T(8,128)(2,1)S(1)}, bf16[40,3072]{1,0:T(8,128)(2,1)S(1)}, u32[]{:S(2)}, u32[]{:S(2)}) %collective-permute-start.16) | collective-permute-done | bytes 245792 | tf_op jit(solution)/shard_map/ppermute | solution.py:48
  30.6 2.6 %collective-permute-done.2.refs_3_ = bf16[40,3072]{1,0:T(8,128)(2,1)S(1)} collective-permute-done((bf16[40,3072]{1,0:T(8,128)(2,1)S(1)}, bf16[40,3072]{1,0:T(8,128)(2,1)S(1)}, u32[]{:S(2)}, u32[]{:S(2)}) %collective-permute-start.2) | collective-permute-done | bytes 245792 | tf_op jit(solution)/shard_map/ppermute | solution.py:48
  35.7 3.3 %collective-permute-start.17 = (bf16[40,3072]{1,0:T(8,128)(2,1)S(1)}, bf16[40,3072]{1,0:T(8,128)(2,1)S(1)}, u32[]{:S(2)}, u32[]{:S(2)}) collective-permute-start(bf16[40,3072]{1,0:T(8,128)(2,1)S(1)} %collective-permute-done.15.refs_1_), channel_id=1, source_target_pairs={{0,12},{1,13},{2,14},{3,15},{4,8},{5,9},{6,10},{7,11},{8,4},{9,5},... | collective-permute-start | bytes 737288 | tf_op jit(solution)/shard_map/ppermute | solution.py:48
  41.5 2.7 %collective-permute-done.17.refs_3_ = bf16[40,3072]{1,0:T(8,128)(2,1)S(1)} collective-permute-done((bf16[40,3072]{1,0:T(8,128)(2,1)S(1)}, bf16[40,3072]{1,0:T(8,128)(2,1)S(1)}, u32[]{:S(2)}, u32[]{:S(2)}) %collective-permute-start.17) | collective-permute-done | bytes 245792 | tf_op jit(solution)/shard_map/ppermute | solution.py:48
  44.2 2.3 %collective-permute-done.19.refs_5_ = bf16[40,3072]{1,0:T(8,128)(2,1)} collective-permute-done((bf16[40,3072]{1,0:T(8,128)(2,1)S(1)}, bf16[40,3072]{1,0:T(8,128)(2,1)}, u32[]{:S(2)}, u32[]{:S(2)}) %collective-permute-start.19) | collective-permute-done | bytes 245792 | tf_op jit(solution)/shard_map/ppermute | solution.py:48
  53.9 5.5 %shard_map.130 = (bf16[640,3072]{1,0:T(8,128)(2,1)S(1)}, bf16[640,512]{1,0:T(8,128)(2,1)S(1)}, f32[640,512]{1,0:T(8,128)S(1)}, f32[640,512]{1,0:T(8,128)S(1)}) custom-call(f32[3]{0:T(128)S(1)} %multiply_exponential_fusion.scales, bf16[3072,512]{1,0:T(8,128)(2,1)S(1)} %shard_map.128.w_gate, bf16[3072,512]{1,0:T(8,128)(2,1)S(1)} %shard_map.129.w_up, ...), custom_call_target="tpu_custom_call" | custom-call | flops 4026531840 | bytes 17432576 | tf_op jit(solution)/shard_map/pallas_call | solution.py:394
  59.5 4.1 %shard_map.131 = (bf16[640,3072]{1,0:T(8,128)(2,1)S(1)}, bf16[256,1536]{1,0:T(8,128)(2,1)S(1)}, bf16[256,1536]{1,0:T(8,128)(2,1)S(1)}, bf16[256,1536]{1,0:T(8,128)(2,1)S(1)}, bf16[256,1536]{1,0:T(8,128)(2,1)S(1)}) custom-call(s32[5]{0:T(128)S(1)} %dynamic-slice_bitcast_fusion.table, bf16[640,512]{1,0:T(8,128)(2,1)S(1)} %get-tuple-element.50.left.hidden, ...), custom_call_target="tpu_custom_call" | custom-call | flops 2013265920 | bytes 7733248 | tf_op jit(solution)/shard_map/pallas_call | solution.py:157
  64.9 2.8 %shard_map.134 = (bf16[640,512]{1,0:T(8,128)(2,1)S(1)}, bf16[640,512]{1,0:T(8,128)(2,1)S(1)}) custom-call(f32[3]{0:T(128)S(1)} %multiply_exponential_fusion.scales, bf16[640,3072]{1,0:T(8,128)(2,1)S(1)} %get-tuple-element.56.scaled, bf16[512,3072]{1,0:T(8,128)(2,1)S(1)} %copy-done, f32[640,512]{1,0:T(8,128)S(1)} %get-tuple-element.57.to_gate, ...), custom_call_target="tpu_custom_call" | custom-call | flops 2013265920 | bytes 11010048 | tf_op jit(solution)/shard_map/pallas_call | solution.py:425
  67.8 3.2 %shard_map.140 = (bf16[256,1536]{1,0:T(8,128)(2,1)S(1)}, bf16[256,1536]{1,0:T(8,128)(2,1)S(1)}, bf16[256,1536]{1,0:T(8,128)(2,1)S(1)}, bf16[256,1536]{1,0:T(8,128)(2,1)S(1)}) custom-call(s32[5]{0:T(128)S(1)} %dynamic-slice_bitcast_fusion.table, bf16[640,512]{1,0:T(8,128)(2,1)S(1)} %get-tuple-element.60.d_up.left, bf16[640,3072]{1,0:T(8,128)(2,1)S(1)} %get-tuple-element.66.right), custom_call_target="tpu_custom_call" | custom-call | flops 2013265920 | bytes 7733248 | tf_op jit(solution)/shard_map/pallas_call | solution.py:193
  73.0 5.0 %shard_map.137 = (bf16[512,1536]{1,0:T(8,128)(2,1)S(1)}, bf16[512,1536]{1,0:T(8,128)(2,1)S(1)}) custom-call(s32[5]{0:T(128)S(1)} %dynamic-slice_bitcast_fusion.table, bf16[640,512]{1,0:T(8,128)(2,1)S(1)} %get-tuple-element.59.d_gate.left, bf16[640,3072]{1,0:T(8,128)(2,1)S(1)} %get-tuple-element.66.right), custom_call_target="tpu_custom_call" | custom-call | flops 2013265920 | bytes 7733248 | tf_op jit(solution)/shard_map/pallas_call | solution.py:228
  78.0 3.0 %collective-permute-start.42 = (bf16[512,1536]{1,0:T(8,128)(2,1)S(1)}, bf16[512,1536]{1,0:T(8,128)(2,1)S(1)}, u32[]{:S(2)}, u32[]{:S(2)}) collective-permute-start(bf16[512,1536]{1,0:T(8,128)(2,1)S(1)} %get-tuple-element.68), channel_id=1, source_target_pairs={{0,16},{16,0},{32,48},{48,32},{64,80},{80,64},{96,112},{112,96},{1... | collective-permute-start | bytes 4718600 | tf_op jit(solution)/shard_map/ppermute | solution.py:52
  82.5 5.4 %shard_map.135 = (bf16[320,3072]{1,0:T(8,128)(2,1)S(1)}, bf16[320,3072]{1,0:T(8,128)(2,1)S(1)}) custom-call(f32[3]{0:T(128)S(1)} %multiply_exponential_fusion.scales, bf16[640,512]{1,0:T(8,128)(2,1)S(1)} %get-tuple-element.59.d_gate.left, bf16[640,512]{1,0:T(8,128)(2,1)S(1)} %get-tuple-element.60.d_up.left, bf16[3072,512]{1,0:T(8,128)(2,1)S(1)} %copy-done.2, ...), custom_call_target="tpu_custom_call" | custom-call | flops 4026531840 | bytes 11534336 | tf_op jit(solution)/shard_map/pallas_call | solution.py:478
  88.9 11.5 %collective-permute-done.47.got_a = bf16[256,1536]{1,0:T(8,128)(2,1)S(1)} collective-permute-done((bf16[256,1536]{1,0:T(8,128)(2,1)S(1)}, bf16[256,1536]{1,0:T(8,128)(2,1)S(1)}, u32[]{:S(2)}, u32[]{:S(2)}) %collective-permute-start.47) | collective-permute-done | bytes 786464 | tf_op jit(solution)/shard_map/ppermute | solution.py:52
  103.2 2.5 %shard_map.132 = (bf16[320,3072]{1,0:T(8,128)(2,1)S(1)}, bf16[320,3072]{1,0:T(8,128)(2,1)S(1)}) custom-call(bf16[640,512]{1,0:T(8,128)(2,1)S(1)} %get-tuple-element.50.left.hidden, bf16[512,3072]{1,0:T(8,128)(2,1)S(1)} %copy-done), custom_call_target="tpu_custom_call" | custom-call | flops 2013265920 | bytes 8257536 | tf_op jit(solution)/shard_map/pallas_call | solution.py:452
  105.8 4.9 %collective-permute-done.54.two_a = bf16[256,768]{1,0:T(8,128)(2,1)S(1)} collective-permute-done((bf16[256,768]{1,0:T(8,128)(2,1)S(1)}, bf16[256,768]{1,0:T(8,128)(2,1)S(1)}, u32[]{:S(2)}, u32[]{:S(2)}) %collective-permute-start.54) | collective-permute-done | bytes 393248 | tf_op jit(solution)/shard_map/ppermute | solution.py:52
  113.7 4.4 %collective-permute-done.49.two_a = bf16[256,768]{1,0:T(8,128)(2,1)S(1)} collective-permute-done((bf16[256,768]{1,0:T(8,128)(2,1)S(1)}, bf16[256,768]{1,0:T(8,128)(2,1)S(1)}, u32[]{:S(2)}, u32[]{:S(2)}) %collective-permute-start.49) | collective-permute-done | bytes 393248 | tf_op jit(solution)/shard_map/ppermute | solution.py:52
  118.1 2.9 %collective-permute-start.56 = (bf16[512,384]{1,0:T(8,128)(2,1)S(1)}, bf16[512,384]{1,0:T(8,128)(2,1)S(1)}, u32[]{:S(2)}, u32[]{:S(2)}) collective-permute-start(bf16[512,384]{1,0:T(8,128)(2,1)S(1)} %get-tuple-element.88), channel_id=1, source_target_pairs={{0,16},{16,0},{32,48},{48,32},{64,80},{80,64},{96,112},{112,96},{1... | collective-permute-start | bytes 1179656 | tf_op jit(solution)/shard_map/ppermute | solution.py:52
  123.5 3.0 %collective-permute-start.51 = (bf16[512,384]{1,0:T(8,128)(2,1)S(1)}, bf16[512,384]{1,0:T(8,128)(2,1)S(1)}, u32[]{:S(2)}, u32[]{:S(2)}) collective-permute-start(bf16[512,384]{1,0:T(8,128)(2,1)S(1)} %get-tuple-element.80), channel_id=1, source_target_pairs={{0,16},{16,0},{32,48},{48,32},{64,80},{80,64},{96,112},{112,96},{1... | collective-permute-start | bytes 1179656 | tf_op jit(solution)/shard_map/ppermute | solution.py:52
  127.5 4.1 %collective-permute-done.56.refs_1_ = bf16[512,384]{1,0:T(8,128)(2,1)S(1)} collective-permute-done((bf16[512,384]{1,0:T(8,128)(2,1)S(1)}, bf16[512,384]{1,0:T(8,128)(2,1)S(1)}, u32[]{:S(2)}, u32[]{:S(2)}) %collective-permute-start.56) | collective-permute-done | bytes 393248 | tf_op jit(solution)/shard_map/ppermute | solution.py:52
  135.6 2.5 %collective-permute-done.51.refs_1_ = bf16[512,384]{1,0:T(8,128)(2,1)S(1)} collective-permute-done((bf16[512,384]{1,0:T(8,128)(2,1)S(1)}, bf16[512,384]{1,0:T(8,128)(2,1)S(1)}, u32[]{:S(2)}, u32[]{:S(2)}) %collective-permute-start.51) | collective-permute-done | bytes 393248 | tf_op jit(solution)/shard_map/ppermute | solution.py:52
  139.7 2.1 %collective-permute-start.46 = (bf16[256,384]{1,0:T(8,128)(2,1)S(1)}, bf16[256,384]{1,0:T(8,128)(2,1)S(1)}, u32[]{:S(2)}, u32[]{:S(2)}) collective-permute-start(bf16[256,384]{1,0:T(8,128)(2,1)S(1)} %add_convert_fusion.7), channel_id=1, source_target_pairs={{0,32},{16,48},{32,0},{48,16},{64,96},{80,112},{96,64},{112,80},{1... | collective-permute-start | bytes 589832 | tf_op jit(solution)/shard_map/ppermute | solution.py:52
  145.8 3.0 %collective-permute-start.33 = (bf16[40,3072]{1,0:T(8,128)(2,1)S(1)}, bf16[40,3072]{1,0:T(8,128)(2,1)S(1)}, u32[]{:S(2)}, u32[]{:S(2)}) collective-permute-start(bf16[40,3072]{1,0:T(8,128)(2,1)S(1)} %get-tuple-element.55), channel_id=1, source_target_pairs={{0,12},{1,13},{2,14},{3,15},{4,8},{5,9},{6,10},{7,11},{8,4},{9,5},... | collective-permute-start | bytes 737288 | tf_op jit(solution)/shard_map/ppermute | solution.py:48
  151.3 3.5 %collective-permute-done.39 = bf16[40,3072]{1,0:T(8,128)(2,1)S(1)} collective-permute-done((bf16[40,3072]{1,0:T(8,128)(2,1)S(1)}, bf16[40,3072]{1,0:T(8,128)(2,1)S(1)}, u32[]{:S(2)}, u32[]{:S(2)}) %collective-permute-start.39) | collective-permute-done | bytes 245792 | tf_op jit(solution)/shard_map/ppermute | solution.py:48
  156.4 3.7 %collective-permute-done.33 = bf16[40,3072]{1,0:T(8,128)(2,1)S(1)} collective-permute-done((bf16[40,3072]{1,0:T(8,128)(2,1)S(1)}, bf16[40,3072]{1,0:T(8,128)(2,1)S(1)}, u32[]{:S(2)}, u32[]{:S(2)}) %collective-permute-start.33) | collective-permute-done | bytes 245792 | tf_op jit(solution)/shard_map/ppermute | solution.py:48
  160.8 9.8 %collective-permute-done.38 = bf16[80,3072]{1,0:T(8,128)(2,1)S(1)} collective-permute-done((bf16[80,3072]{1,0:T(8,128)(2,1)S(1)}, bf16[80,3072]{1,0:T(8,128)(2,1)S(1)}, u32[]{:S(2)}, u32[]{:S(2)}) %collective-permute-start.38) | collective-permute-done | bytes 491552 | tf_op jit(solution)/shard_map/ppermute | solution.py:48
  171.2 6.5 %collective-permute-done.32 = bf16[80,3072]{1,0:T(8,128)(2,1)S(1)} collective-permute-done((bf16[80,3072]{1,0:T(8,128)(2,1)S(1)}, bf16[80,3072]{1,0:T(8,128)(2,1)S(1)}, u32[]{:S(2)}, u32[]{:S(2)}) %collective-permute-start.32) | collective-permute-done | bytes 491552 | tf_op jit(solution)/shard_map/ppermute | solution.py:48
  179.0 5.1 %collective-permute-done.35 = bf16[40,3072]{1,0:T(8,128)(2,1)S(1)} collective-permute-done((bf16[40,3072]{1,0:T(8,128)(2,1)S(1)}, bf16[40,3072]{1,0:T(8,128)(2,1)S(1)}, u32[]{:S(2)}, u32[]{:S(2)}) %collective-permute-start.35) | collective-permute-done | bytes 245792 | tf_op jit(solution)/shard_map/ppermute | solution.py:48
  (144 shorter events, 54.1 us)
Async XLA Ops:
  2.3 10.9 %collective-permute-start.5 = (bf16[40,3072]{1,0:T(8,128)(2,1)}, bf16[40,3072]{1,0:T(8,128)(2,1)S(1)}, u32[]{:S(2)}, u32[]{:S(2)}) collective-permute-start(bf16[40,3072]{1,0:T(8,128)(2,1)} %refs_0_.5), channel_id=1, source_target_pairs={{0,8},{1,9},{2,10},{3,11},{4,12},{5,13},{6,14},{7,15},{8,0},{9,1},... | collective-permute-start | bytes 737288 | tf_op jit(solution)/shard_map/ppermute | solution.py:48
  6.2 13.3 %collective-permute-start.3 = (bf16[40,3072]{1,0:T(8,128)(2,1)}, bf16[40,3072]{1,0:T(8,128)(2,1)S(1)}, u32[]{:S(2)}, u32[]{:S(2)}) collective-permute-start(bf16[40,3072]{1,0:T(8,128)(2,1)} %refs_0_.5), channel_id=1, source_target_pairs={{0,4},{1,5},{2,6},{3,7},{4,0},{5,1},{6,2},{7,3},{8,12},{9,13},{10,... | collective-permute-start | bytes 737288 | tf_op jit(solution)/shard_map/ppermute | solution.py:48
  7.2 12.3 %collective-permute-start.1 = (bf16[40,3072]{1,0:T(8,128)(2,1)}, bf16[40,3072]{1,0:T(8,128)(2,1)S(1)}, u32[]{:S(2)}, u32[]{:S(2)}) collective-permute-start(bf16[40,3072]{1,0:T(8,128)(2,1)} %refs_0_.5), channel_id=1, source_target_pairs={{0,12},{1,13},{2,14},{3,15},{4,8},{5,9},{6,10},{7,11},{8,4},{9,5},... | collective-permute-start | bytes 737288 | tf_op jit(solution)/shard_map/ppermute | solution.py:48
  7.2 13.4 %collective-permute-start.7 = (bf16[40,3072]{1,0:T(8,128)(2,1)}, bf16[40,3072]{1,0:T(8,128)(2,1)S(1)}, u32[]{:S(2)}, u32[]{:S(2)}) collective-permute-start(bf16[40,3072]{1,0:T(8,128)(2,1)} %refs_0_.5), channel_id=1, source_target_pairs={{0,1},{1,0},{2,3},{3,2},{4,5},{5,4},{6,7},{7,6},{8,9},{9,8},{10,11... | collective-permute-start | bytes 737288 | tf_op jit(solution)/shard_map/ppermute | solution.py:48
  9.0 11.7 %collective-permute-start.15 = (bf16[40,3072]{1,0:T(8,128)(2,1)S(1)}, bf16[40,3072]{1,0:T(8,128)(2,1)S(1)}, u32[]{:S(2)}, u32[]{:S(2)}) collective-permute-start(bf16[40,3072]{1,0:T(8,128)(2,1)S(1)} %multiply_convert_fusion.1.refs_0_), channel_id=1, source_target_pairs={{0,2},{1,3},{2,0},{3,1},{4,6},{5,7},{6,4},{7,5},{8,10},{9,11},{10,... | collective-permute-start | bytes 737288 | tf_op jit(solution)/shard_map/ppermute | solution.py:48
  13.2 10.1 %collective-permute-start.20 = (bf16[40,3072]{1,0:T(8,128)(2,1)S(1)}, bf16[40,3072]{1,0:T(8,128)(2,1)S(1)}, u32[]{:S(2)}, u32[]{:S(2)}) collective-permute-start(bf16[40,3072]{1,0:T(8,128)(2,1)S(1)} %multiply_convert_fusion.1.refs_0_), channel_id=1, source_target_pairs={{0,8},{1,9},{2,10},{3,11},{4,12},{5,13},{6,14},{7,15},{8,0},{9,1},... | collective-permute-start | bytes 737288 | tf_op jit(solution)/shard_map/ppermute | solution.py:48
  19.5 10.6 %collective-permute-start.18 = (bf16[40,3072]{1,0:T(8,128)(2,1)S(1)}, bf16[40,3072]{1,0:T(8,128)(2,1)S(1)}, u32[]{:S(2)}, u32[]{:S(2)}) collective-permute-start(bf16[40,3072]{1,0:T(8,128)(2,1)S(1)} %multiply_convert_fusion.1.refs_0_), channel_id=1, source_target_pairs={{0,4},{1,5},{2,6},{3,7},{4,0},{5,1},{6,2},{7,3},{8,12},{9,13},{10,... | collective-permute-start | bytes 737288 | tf_op jit(solution)/shard_map/ppermute | solution.py:48
  20.6 12.5 %collective-permute-start.2 = (bf16[40,3072]{1,0:T(8,128)(2,1)S(1)}, bf16[40,3072]{1,0:T(8,128)(2,1)S(1)}, u32[]{:S(2)}, u32[]{:S(2)}) collective-permute-start(bf16[40,3072]{1,0:T(8,128)(2,1)S(1)} %collective-permute-done.refs_1_), channel_id=1, source_target_pairs={{0,12},{1,13},{2,14},{3,15},{4,8},{5,9},{6,10},{7,11},{8,4},{9,5},... | collective-permute-start | bytes 737288 | tf_op jit(solution)/shard_map/ppermute | solution.py:48
  23.3 10.6 %collective-permute-start.4 = (bf16[40,3072]{1,0:T(8,128)(2,1)S(1)}, bf16[40,3072]{1,0:T(8,128)(2,1)S(1)}, u32[]{:S(2)}, u32[]{:S(2)}) collective-permute-start(bf16[40,3072]{1,0:T(8,128)(2,1)S(1)} %collective-permute-done.refs_1_), channel_id=1, source_target_pairs={{0,4},{1,5},{2,6},{3,7},{4,0},{5,1},{6,2},{7,3},{8,12},{9,13},{10,... | collective-permute-start | bytes 737288 | tf_op jit(solution)/shard_map/ppermute | solution.py:48
  40.9 11.4 %collective-permute-start.23 = (bf16[40,3072]{1,0:T(8,128)(2,1)S(1)}, bf16[40,3072]{1,0:T(8,128)(2,1)S(1)}, u32[]{:S(2)}, u32[]{:S(2)}) collective-permute-start(bf16[40,3072]{1,0:T(8,128)(2,1)S(1)} %collective-permute-done.15.refs_1_), channel_id=1, source_target_pairs={{0,1},{1,0},{2,3},{3,2},{4,5},{5,4},{6,7},{7,6},{8,9},{9,8},{10,11... | collective-permute-start | bytes 737288 | tf_op jit(solution)/shard_map/ppermute | solution.py:48
  41.0 11.9 %collective-permute-start.28 = (bf16[40,3072]{1,0:T(8,128)(2,1)S(1)}, bf16[40,3072]{1,0:T(8,128)(2,1)S(1)}, u32[]{:S(2)}, u32[]{:S(2)}) collective-permute-start(bf16[40,3072]{1,0:T(8,128)(2,1)S(1)} %collective-permute-done.20.refs_6_), channel_id=1, source_target_pairs={{0,1},{1,0},{2,3},{3,2},{4,5},{5,4},{6,7},{7,6},{8,9},{9,8},{10,11... | collective-permute-start | bytes 737288 | tf_op jit(solution)/shard_map/ppermute | solution.py:48
  63.7 24.3 %collective-permute-start.52 = (bf16[256,1536]{1,0:T(8,128)(2,1)S(1)}, bf16[256,1536]{1,0:T(8,128)(2,1)S(1)}, u32[]{:S(2)}, u32[]{:S(2)}) collective-permute-start(bf16[256,1536]{1,0:T(8,128)(2,1)S(1)} %get-tuple-element.82), channel_id=1, source_target_pairs={{0,32},{16,48},{32,0},{48,16},{64,96},{80,112},{96,64},{112,80},{1... | collective-permute-start | bytes 2359304 | tf_op jit(solution)/shard_map/ppermute | solution.py:52
  64.9 23.1 %collective-permute-start.53 = (bf16[256,1536]{1,0:T(8,128)(2,1)S(1)}, bf16[256,1536]{1,0:T(8,128)(2,1)S(1)}, u32[]{:S(2)}, u32[]{:S(2)}) collective-permute-start(bf16[256,1536]{1,0:T(8,128)(2,1)S(1)} %get-tuple-element.84), channel_id=1, source_target_pairs={{0,96},{16,112},{32,64},{48,80},{64,32},{80,48},{96,0},{112,16},{1... | collective-permute-start | bytes 2359304 | tf_op jit(solution)/shard_map/ppermute | solution.py:52
  71.0 29.4 %collective-permute-start.47 = (bf16[256,1536]{1,0:T(8,128)(2,1)S(1)}, bf16[256,1536]{1,0:T(8,128)(2,1)S(1)}, u32[]{:S(2)}, u32[]{:S(2)}) collective-permute-start(bf16[256,1536]{1,0:T(8,128)(2,1)S(1)} %get-tuple-element.74), channel_id=1, source_target_pairs={{0,32},{16,48},{32,0},{48,16},{64,96},{80,112},{96,64},{112,80},{1... | collective-permute-start | bytes 2359304 | tf_op jit(solution)/shard_map/ppermute | solution.py:52
  78.0 48.4 %collective-permute-start.42 = (bf16[512,1536]{1,0:T(8,128)(2,1)S(1)}, bf16[512,1536]{1,0:T(8,128)(2,1)S(1)}, u32[]{:S(2)}, u32[]{:S(2)}) collective-permute-start(bf16[512,1536]{1,0:T(8,128)(2,1)S(1)} %get-tuple-element.68), channel_id=1, source_target_pairs={{0,16},{16,0},{32,48},{48,32},{64,80},{80,64},{96,112},{112,96},{1... | collective-permute-start | bytes 4718600 | tf_op jit(solution)/shard_map/ppermute | solution.py:52
  81.0 21.2 %collective-permute-start.48 = (bf16[256,1536]{1,0:T(8,128)(2,1)S(1)}, bf16[256,1536]{1,0:T(8,128)(2,1)S(1)}, u32[]{:S(2)}, u32[]{:S(2)}) collective-permute-start(bf16[256,1536]{1,0:T(8,128)(2,1)S(1)} %get-tuple-element.76), channel_id=1, source_target_pairs={{0,96},{16,112},{32,64},{48,80},{64,32},{80,48},{96,0},{112,16},{1... | collective-permute-start | bytes 2359304 | tf_op jit(solution)/shard_map/ppermute | solution.py:52
  88.0 54.5 %collective-permute-start.36 = (bf16[320,3072]{1,0:T(8,128)(2,1)S(1)}, bf16[320,3072]{1,0:T(8,128)(2,1)S(1)}, u32[]{:S(2)}, u32[]{:S(2)}) collective-permute-start(bf16[320,3072]{1,0:T(8,128)(2,1)S(1)} %get-tuple-element.62), channel_id=1, source_target_pairs={{0,1},{1,0},{2,3},{3,2},{4,5},{5,4},{6,7},{7,6},{8,9},{9,8},{10,11... | collective-permute-start | bytes 5898248 | tf_op jit(solution)/shard_map/ppermute | solution.py:48
  88.3 22.4 %collective-permute-start.54 = (bf16[256,768]{1,0:T(8,128)(2,1)S(1)}, bf16[256,768]{1,0:T(8,128)(2,1)S(1)}, u32[]{:S(2)}, u32[]{:S(2)}) collective-permute-start(bf16[256,768]{1,0:T(8,128)(2,1)S(1)} %get-tuple-element.85), channel_id=1, source_target_pairs={{0,96},{16,112},{32,64},{48,80},{64,32},{80,48},{96,0},{112,16},{1... | collective-permute-start | bytes 1179656 | tf_op jit(solution)/shard_map/ppermute | solution.py:52
  100.3 10.4 %collective-permute-start.55 = (bf16[256,768]{1,0:T(8,128)(2,1)S(1)}, bf16[256,768]{1,0:T(8,128)(2,1)S(1)}, u32[]{:S(2)}, u32[]{:S(2)}) collective-permute-start(bf16[256,768]{1,0:T(8,128)(2,1)S(1)} %get-tuple-element.86), channel_id=1, source_target_pairs={{0,32},{16,48},{32,0},{48,16},{64,96},{80,112},{96,64},{112,80},{1... | collective-permute-start | bytes 1179656 | tf_op jit(solution)/shard_map/ppermute | solution.py:52
  102.4 15.7 %collective-permute-start.49 = (bf16[256,768]{1,0:T(8,128)(2,1)S(1)}, bf16[256,768]{1,0:T(8,128)(2,1)S(1)}, u32[]{:S(2)}, u32[]{:S(2)}) collective-permute-start(bf16[256,768]{1,0:T(8,128)(2,1)S(1)} %get-tuple-element.77), channel_id=1, source_target_pairs={{0,96},{16,112},{32,64},{48,80},{64,32},{80,48},{96,0},{112,16},{1... | collective-permute-start | bytes 1179656 | tf_op jit(solution)/shard_map/ppermute | solution.py:52
  110.6 34.5 %collective-permute-start.30 = (bf16[320,3072]{1,0:T(8,128)(2,1)S(1)}, bf16[320,3072]{1,0:T(8,128)(2,1)S(1)}, u32[]{:S(2)}, u32[]{:S(2)}) collective-permute-start(bf16[320,3072]{1,0:T(8,128)(2,1)S(1)} %get-tuple-element.52), channel_id=1, source_target_pairs={{0,1},{1,0},{2,3},{3,2},{4,5},{5,4},{6,7},{7,6},{8,9},{9,8},{10,11... | collective-permute-start | bytes 5898248 | tf_op jit(solution)/shard_map/ppermute | solution.py:48
  110.7 11.8 %collective-permute-start.50 = (bf16[256,768]{1,0:T(8,128)(2,1)S(1)}, bf16[256,768]{1,0:T(8,128)(2,1)S(1)}, u32[]{:S(2)}, u32[]{:S(2)}) collective-permute-start(bf16[256,768]{1,0:T(8,128)(2,1)S(1)} %get-tuple-element.78), channel_id=1, source_target_pairs={{0,32},{16,48},{32,0},{48,16},{64,96},{80,112},{96,64},{112,80},{1... | collective-permute-start | bytes 1179656 | tf_op jit(solution)/shard_map/ppermute | solution.py:52
  118.1 13.5 %collective-permute-start.56 = (bf16[512,384]{1,0:T(8,128)(2,1)S(1)}, bf16[512,384]{1,0:T(8,128)(2,1)S(1)}, u32[]{:S(2)}, u32[]{:S(2)}) collective-permute-start(bf16[512,384]{1,0:T(8,128)(2,1)S(1)} %get-tuple-element.88), channel_id=1, source_target_pairs={{0,16},{16,0},{32,48},{48,32},{64,80},{80,64},{96,112},{112,96},{1... | collective-permute-start | bytes 1179656 | tf_op jit(solution)/shard_map/ppermute | solution.py:52
  123.5 14.6 %collective-permute-start.51 = (bf16[512,384]{1,0:T(8,128)(2,1)S(1)}, bf16[512,384]{1,0:T(8,128)(2,1)S(1)}, u32[]{:S(2)}, u32[]{:S(2)}) collective-permute-start(bf16[512,384]{1,0:T(8,128)(2,1)S(1)} %get-tuple-element.80), channel_id=1, source_target_pairs={{0,16},{16,0},{32,48},{48,32},{64,80},{80,64},{96,112},{112,96},{1... | collective-permute-start | bytes 1179656 | tf_op jit(solution)/shard_map/ppermute | solution.py:52
  126.9 12.7 %collective-permute-start.45 = (bf16[256,768]{1,0:T(8,128)(2,1)S(1)}, bf16[256,768]{1,0:T(8,128)(2,1)S(1)}, u32[]{:S(2)}, u32[]{:S(2)}) collective-permute-start(bf16[256,768]{1,0:T(8,128)(2,1)S(1)} %get-tuple-element.72), channel_id=1, source_target_pairs={{0,96},{16,112},{32,64},{48,80},{64,32},{80,48},{96,0},{112,16},{1... | collective-permute-start | bytes 1179656 | tf_op jit(solution)/shard_map/ppermute | solution.py:52
  131.6 10.2 %collective-permute-start.43 = (bf16[256,768]{1,0:T(8,128)(2,1)S(1)}, bf16[256,768]{1,0:T(8,128)(2,1)S(1)}, u32[]{:S(2)}, u32[]{:S(2)}) collective-permute-start(bf16[256,768]{1,0:T(8,128)(2,1)S(1)} %get-tuple-element.70), channel_id=1, source_target_pairs={{0,32},{16,48},{32,0},{48,16},{64,96},{80,112},{96,64},{112,80},{1... | collective-permute-start | bytes 1179656 | tf_op jit(solution)/shard_map/ppermute | solution.py:52
  145.6 10.8 %collective-permute-start.31 = (bf16[40,3072]{1,0:T(8,128)(2,1)S(1)}, bf16[40,3072]{1,0:T(8,128)(2,1)S(1)}, u32[]{:S(2)}, u32[]{:S(2)}) collective-permute-start(bf16[40,3072]{1,0:T(8,128)(2,1)S(1)} %get-tuple-element.54), channel_id=1, source_target_pairs={{0,4},{1,5},{2,6},{3,7},{4,0},{5,1},{6,2},{7,3},{8,12},{9,13},{10,... | collective-permute-start | bytes 737288 | tf_op jit(solution)/shard_map/ppermute | solution.py:48
  145.8 14.3 %collective-permute-start.33 = (bf16[40,3072]{1,0:T(8,128)(2,1)S(1)}, bf16[40,3072]{1,0:T(8,128)(2,1)S(1)}, u32[]{:S(2)}, u32[]{:S(2)}) collective-permute-start(bf16[40,3072]{1,0:T(8,128)(2,1)S(1)} %get-tuple-element.55), channel_id=1, source_target_pairs={{0,12},{1,13},{2,14},{3,15},{4,8},{5,9},{6,10},{7,11},{8,4},{9,5},... | collective-permute-start | bytes 737288 | tf_op jit(solution)/shard_map/ppermute | solution.py:48
  155.0 15.6 %collective-permute-start.38 = (bf16[80,3072]{1,0:T(8,128)(2,1)S(1)}, bf16[80,3072]{1,0:T(8,128)(2,1)S(1)}, u32[]{:S(2)}, u32[]{:S(2)}) collective-permute-start(bf16[80,3072]{1,0:T(8,128)(2,1)S(1)} %pad_maximum_fusion.2), channel_id=1, source_target_pairs={{0,12},{1,13},{2,14},{3,15},{4,8},{5,9},{6,10},{7,11},{8,4},{9,5},... | collective-permute-start | bytes 1474568 | tf_op jit(solution)/shard_map/ppermute | solution.py:48
  155.4 15.2 %collective-permute-start.40 = (bf16[80,3072]{1,0:T(8,128)(2,1)S(1)}, bf16[80,3072]{1,0:T(8,128)(2,1)S(1)}, u32[]{:S(2)}, u32[]{:S(2)}) collective-permute-start(bf16[80,3072]{1,0:T(8,128)(2,1)S(1)} %pad_maximum_fusion.3), channel_id=1, source_target_pairs={{0,4},{1,5},{2,6},{3,7},{4,0},{5,1},{6,2},{7,3},{8,12},{9,13},{10,... | collective-permute-start | bytes 1474568 | tf_op jit(solution)/shard_map/ppermute | solution.py:48
  160.2 17.4 %collective-permute-start.32 = (bf16[80,3072]{1,0:T(8,128)(2,1)S(1)}, bf16[80,3072]{1,0:T(8,128)(2,1)S(1)}, u32[]{:S(2)}, u32[]{:S(2)}) collective-permute-start(bf16[80,3072]{1,0:T(8,128)(2,1)S(1)} %pad_maximum_fusion), channel_id=1, source_target_pairs={{0,12},{1,13},{2,14},{3,15},{4,8},{5,9},{6,10},{7,11},{8,4},{9,5},... | collective-permute-start | bytes 1474568 | tf_op jit(solution)/shard_map/ppermute | solution.py:48
  160.7 17.0 %collective-permute-start.34 = (bf16[80,3072]{1,0:T(8,128)(2,1)S(1)}, bf16[80,3072]{1,0:T(8,128)(2,1)S(1)}, u32[]{:S(2)}, u32[]{:S(2)}) collective-permute-start(bf16[80,3072]{1,0:T(8,128)(2,1)S(1)} %pad_maximum_fusion.1), channel_id=1, source_target_pairs={{0,4},{1,5},{2,6},{3,7},{4,0},{5,1},{6,2},{7,3},{8,12},{9,13},{10,... | collective-permute-start | bytes 1474568 | tf_op jit(solution)/shard_map/ppermute | solution.py:48
  (37 other events, 222.9 us)
